TPU v7x, 128 devices: a whole 4x4x4 slice. The times are simulated.
128 devices in a mesh: bulk: 8 (over x, core), valve: 16 (over z, y).
Axes of the slice: x: 4, y: 4, z: 4, core: 2. Of those that a mesh axis runs over, the one named last changes fastest.
Arguments:
- bg_adjoint: float32 [5, 64, 512, 128], P(None, 'bulk', 'valve'), may hold values from -6 to 6
- bg_velocity: float32 [3, 64, 512, 128], P(None, 'bulk', 'valve'), may hold values from -6 to 6
- bg_source: float32 [5, 64, 512, 128], P(None, 'bulk', 'valve'), may hold values from -6 to 6
- bg_iblank: int32 [64, 512, 128], P('bulk', 'valve'), may hold values 0 or 1
- valve_adjoint: float32 [5, 128, 256, 128], P(None, 'valve', 'bulk'), may hold values from -6 to 6
- valve_velocity: float32 [3, 128, 256, 128], P(None, 'valve', 'bulk'), may hold values from -6 to 6
- valve_source: float32 [5, 128, 256, 128], P(None, 'valve', 'bulk'), may hold values from -6 to 6
- flux_mix: float32 [3, 5, 5], replicated, may hold values from -2.5 to 2.5
- rec_cell: int32 [128, 128, 128], P(('bulk', 'valve')), may hold values from 0 to 32767
- donor_base: int32 [128, 128, 128], P(('bulk', 'valve')), may hold values from 0 to 28542, as said below
- donor_weight: float32 [8, 128, 128, 128], P(None, ('bulk', 'valve')), may hold values from 0 to 1, as said below
- slot_count: int32 [128, 128], P(('bulk', 'valve')), may hold values from 0 to 128, as said below
Outputs:
- bg_out: float32 [5, 64, 512, 128], P(None, 'bulk', 'valve')
- valve_out: float32 [5, 128, 256, 128], P(None, 'valve', 'bulk')
Inputs may be any that keep to these rules, and one draw needn't show every extreme that they name: donor_base is a cell of the block whose neighbours at +1 along each of the three dimensions, alone and together, are in the same block; both ends of the range occur in every draw. `donor_weight`: the eight weights of a slot are non-negative and sum to one. `slot_count`: some owner takes 128 live slots from every sender.
All inputs are finite; a program needn't handle non-finite values. No bound on the sum of `bg_iblank` on one device may be relied on, other than what follows from the above.
Results may differ from a plain program's by a relative error of at most 0.0001.
Values sent between devices are 32-bit elements; how exact they have to be, the bound alone decides.
A program may use at most 128 MiB of HBM per device.

v0:
```python
import functools

import jax
import jax.numpy as jnp
from jax import lax
from jax.experimental import pallas as pl
from jax.experimental.pallas import tpu as pltpu
from jax.sharding import PartitionSpec as P

NVAR = 5
ITERS = 4
CAP = 128
BX = 8
BY = 32
BZ = 128
PLANES = BX * BY
GROUP = 16

f32 = jnp.float32
bf16 = jnp.bfloat16
NT = (((1,), (1,)), ((), ()))
NN = (((1,), (0,)), ((), ()))
MESH = pl.DeviceIdType.MESH


def sweep_kernel(*refs):
    (flux_ref, valve_adj, valve_vel, valve_src, bg_adj, bg_vel, bg_src, bg_blank, valve_out, bg_out) = refs[:10]
    fields = (refs[10 : 10 + ITERS], refs[10 + ITERS : 10 + 2 * ITERS])
    (slopes, scale, edge_in, edge_out, load_sem, send_sem, recv_sem) = refs[10 + 2 * ITERS :]
    bulk, valve = lax.axis_index("bulk"), lax.axis_index("valve")
    n_bulk, n_valve = lax.axis_size("bulk"), lax.axis_size("valve")
    place = {"bulk": (bulk, n_bulk), "valve": (valve, n_valve)}
    axes = (("valve", "bulk"), ("bulk", "valve"))
    inputs = ((valve_adj, valve_vel, valve_src), (bg_adj, bg_vel, bg_src))
    outputs = (valve_out, bg_out)

    loads = [
        pltpu.make_async_copy(inputs[g][0], fields[g][0].at[:, pl.ds(1, BX)], load_sem.at[g])
        for g in range(2)
    ]
    for load in loads:
        load.start()

    def clear(g, side):
        index, count = place[axes[g][0]]

        @pl.when(index == (0 if side == 0 else count - 1))
        def _():
            for t in range(ITERS):
                fields[g][t][:, (BX + 1) * side] = jnp.zeros((NVAR, BY, BZ), f32)

        index, count = place[axes[g][1]]

        @pl.when(index == (0 if side == 0 else count - 1))
        def _():
            for t in range(ITERS):
                edge_in[g, t, side] = jnp.zeros((NVAR, BX, 1, BZ), f32)

    for g in range(2):
        for side in range(2):
            clear(g, side)

    barrier = pltpu.get_barrier_semaphore()
    for axis in ("bulk", "valve"):
        index, count = place[axis]
        for step in (1, count - 1):
            pl.semaphore_signal(
                barrier, inc=1, device_id={axis: lax.rem(index + step, count)}, device_id_type=MESH
            )

    def slope_rows(x, carry):
        for g in range(2):
            parts = [inputs[g][1][d, x] for d in range(3)]
            square = parts[0] * parts[0] + parts[1] * parts[1] + parts[2] * parts[2]
            half = 0.5 * lax.rsqrt(1.0 + square)
            for d in range(3):
                slopes[g, d, x] = parts[d] * half
        scale[x] = bg_blank[x].astype(f32) * (1.0 / 12.0)
        return carry

    def copies(g, t, side):
        away = 1 - side
        found = []
        for kind in range(2):
            index, count = place[axes[g][kind]]
            target = lax.rem(index + (1 if side else count - 1), count)
            if kind == 0:
                source = fields[g][t].at[:, BX if side else 1]
                landing = fields[g][t].at[:, 0 if side else BX + 1]
            else:
                source = edge_out.at[g, t, side]
                landing = edge_in.at[g, t, away]
            found.append(
                (
                    index < count - 1 if side else index > 0,
                    index > 0 if side else index < count - 1,
                    pltpu.make_async_remote_copy(
                        src_ref=source,
                        dst_ref=landing,
                        send_sem=send_sem.at[g, t, side, kind],
                        recv_sem=recv_sem.at[g, t, side, kind],
                        device_id={axes[g][kind]: target},
                        device_id_type=MESH,
                    ),
                )
            )
        return found

    def send(g, t):
        for side in range(2):
            for sends, _, copy in copies(g, t, side):
                pl.when(sends)(copy.start)

    def arrive(g, t):
        for side in range(2):
            for _, receives, copy in copies(g, t, side):
                pl.when(receives)(copy.wait_recv)

    def left(g, t):
        for side in range(2):
            for sends, _, copy in copies(g, t, side):
                pl.when(sends)(copy.wait_send)

    row = lax.broadcasted_iota(jnp.int32, (BY, BZ), 0)
    lane = lax.broadcasted_iota(jnp.int32, (BY, BZ), 1)

    def sweep(g, t):
        now = fields[g][t]
        source = inputs[g][2]

        def rows(x, carry):
            around, steep = [], [[], [], []]
            for c in range(NVAR):
                here = now[c, x + 1]
                x_low, x_high = now[c, x], now[c, x + 2]
                y_low = jnp.where(row == 0, edge_in[g, t, 0, c, x], pltpu.roll(here, 1, axis=0))
                y_high = jnp.where(row == BY - 1, edge_in[g, t, 1, c, x], pltpu.roll(here, BY - 1, axis=0))
                z_low = jnp.where(lane == 0, 0.0, pltpu.roll(here, 1, axis=1))
                z_high = jnp.where(lane == BZ - 1, 0.0, pltpu.roll(here, BZ - 1, axis=1))
                around.append(
                    (x_low + x_high) + (y_low + y_high) + (z_low + z_high) + source[c, x]
                )
                for d, (low, high) in enumerate(((x_low, x_high), (y_low, y_high), (z_low, z_high))):
                    steep[d].append(slopes[g, d, x] * (low - high))
            factor = scale[x] if g else 1.0 / 12.0
            for i in range(NVAR):
                total = around[i]
                for d in range(3):
                    for j in range(NVAR):
                        total = total - flux_ref[d, j, i] * steep[d][j]
                total = total * factor
                if t == ITERS - 1:
                    outputs[g][i, x] = total
                else:
                    fields[g][t + 1][i, x + 1] = total
                    edge_out[g, t + 1, 0, i, x] = total[0:1]
                    edge_out[g, t + 1, 1, i, x] = total[BY - 1 : BY]
            return carry

        lax.fori_loop(0, BX, rows, 0)

    def first_edges(g):
        def rows(x, carry):
            for c in range(NVAR):
                here = fields[g][0][c, x + 1]
                edge_out[g, 0, 0, c, x] = here[0:1]
                edge_out[g, 0, 1, c, x] = here[BY - 1 : BY]
            return carry

        lax.fori_loop(0, BX, rows, 0)

    for g in range(2):
        loads[g].wait()
        first_edges(g)
    pl.semaphore_wait(barrier, 4)
    for g in range(2):
        send(g, 0)
    lax.fori_loop(0, BX, slope_rows, 0)
    for t in range(ITERS):
        for g in range(2):
            arrive(g, t)
            sweep(g, t)
            if t + 1 < ITERS:
                send(g, t + 1)
    for t in range(ITERS):
        for g in range(2):
            left(g, t)


def sweep_grids(flux_mix, valve_adj, valve_vel, valve_src, bg_adj, bg_vel, bg_src, bg_blank):
    whole = pl.BlockSpec(memory_space=pltpu.VMEM)
    far = pl.BlockSpec(memory_space=pl.ANY)
    out = jax.ShapeDtypeStruct(valve_adj.shape, f32)
    edges = pltpu.VMEM((2, ITERS, 2, NVAR, BX, 1, BZ), f32)
    return pl.pallas_call(
        sweep_kernel,
        out_shape=(out, out),
        in_specs=[pl.BlockSpec(memory_space=pltpu.SMEM), far, whole, whole, far, whole, whole, whole],
        out_specs=(whole, whole),
        scratch_shapes=[pltpu.VMEM((NVAR, BX + 2, BY, BZ), f32)] * (2 * ITERS)
        + [
            pltpu.VMEM((2, 3, BX, BY, BZ), f32),
            pltpu.VMEM((BX, BY, BZ), f32),
            edges,
            edges,
            pltpu.SemaphoreType.DMA((2,)),
            pltpu.SemaphoreType.DMA((2, ITERS, 2, 2)),
            pltpu.SemaphoreType.DMA((2, ITERS, 2, 2)),
        ],
        compiler_params=pltpu.CompilerParams(
            collective_id=0, has_side_effects=True, vmem_limit_bytes=56 * 2**20
        ),
    )(flux_mix, valve_adj, valve_vel, valve_src, bg_adj, bg_vel, bg_src, bg_blank)


def split(x):
    hi = x.astype(bf16)
    return hi, (x - hi.astype(f32)).astype(bf16)


def as_bf16(x):
    return x.astype(f32).astype(bf16)


def pick_kernel(count_ref, cell_ref, field_ref, out_ref, table):
    for c in range(NVAR):
        hi, lo = split(field_ref[c].T)
        table[pl.ds(c * BZ, BZ), 0:PLANES] = hi
        table[pl.ds(c * BZ, BZ), PLANES : 2 * PLANES] = lo
    plane_row = as_bf16(lax.broadcasted_iota(jnp.int32, (PLANES, CAP), 0))
    depth_row = lax.broadcasted_iota(jnp.int32, (BZ, CAP), 0)
    slot = lax.broadcasted_iota(jnp.int32, (1, CAP), 1)
    one, zero = jnp.ones((), bf16), jnp.zeros((), bf16)

    def body(block, carry):
        hits, depths = [], []
        for u in range(GROUP):
            owner = block * GROUP + u
            cell = cell_ref[owner]
            hits.append(jnp.where(plane_row == as_bf16(cell >> 7), one, zero))
            depths.append(jnp.where(slot < count_ref[0, owner], cell & (BZ - 1), -1))
        hits = jnp.concatenate(hits, axis=1)
        columns = lax.dot_general(
            table[...], jnp.concatenate([hits, hits], axis=0), NN, preferred_element_type=f32
        )
        for u in range(GROUP):
            here = depth_row == depths[u]
            rows = [
                jnp.sum(
                    jnp.where(here, columns[c * BZ : (c + 1) * BZ, u * CAP : (u + 1) * CAP], 0.0),
                    axis=0,
                    keepdims=True,
                )
                for c in range(NVAR)
            ]
            out_ref[block * GROUP + u] = jnp.concatenate(rows + [jnp.zeros((3, CAP), f32)], axis=0)
        return carry

    lax.fori_loop(0, out_ref.shape[0] // GROUP, body, 0)


def pick(field, cells, counts):
    owners = cells.shape[0]
    return pl.pallas_call(
        pick_kernel,
        out_shape=jax.ShapeDtypeStruct((owners, 8, CAP), f32),
        in_specs=[
            pl.BlockSpec(memory_space=pltpu.SMEM),
            pl.BlockSpec(memory_space=pltpu.VMEM),
            pl.BlockSpec(memory_space=pltpu.VMEM),
        ],
        out_specs=pl.BlockSpec(memory_space=pltpu.VMEM),
        scratch_shapes=[pltpu.VMEM((NVAR * BZ, 2 * PLANES), bf16)],
        compiler_params=pltpu.CompilerParams(vmem_limit_bytes=56 * 2**20),
    )(counts, cells.reshape(owners, 1, CAP), field.reshape(NVAR, PLANES, BZ))


def push_kernel(value_ref, weight_ref, base_ref, field_ref, out_ref, total):
    total[...] = jnp.zeros_like(total)
    plane_row = as_bf16(lax.broadcasted_iota(jnp.int32, (PLANES, CAP), 0))
    depth_row = as_bf16(lax.broadcasted_iota(jnp.int32, (BZ, CAP), 0))
    zero = jnp.zeros((), bf16)

    def terms(sender):
        base = base_ref[sender]
        plane = base >> 7
        weight_hi, weight_lo = split(weight_ref[sender])
        value_hi, value_lo = split(value_ref[sender])
        hits = [plane_row == as_bf16(plane + off) for off in (0, 1, BY, BY + 1)]

        def spread(weight):
            halves = []
            for step in range(2):
                rows = jnp.zeros((PLANES, CAP), bf16)
                for pair in range(4):
                    rows = jnp.where(hits[pair], weight[2 * pair + step : 2 * pair + step + 1], rows)
                halves.append(rows)
            return jnp.concatenate(halves, axis=0)

        here = depth_row == as_bf16(base & (BZ - 1))

        def placed(value):
            return jnp.concatenate(
                [jnp.where(here, value[c : c + 1], zero) for c in range(NVAR)], axis=0
            )

        return spread(weight_hi), spread(weight_lo), placed(value_hi), placed(value_lo)

    def body(block, carry):
        parts = [terms(block * GROUP + u) for u in range(GROUP)]
        spread_hi, spread_lo, placed_hi, placed_lo = [[part[i] for part in parts] for i in range(4)]
        spread = jnp.concatenate(spread_hi + spread_hi + spread_lo, axis=1)
        placed = jnp.concatenate(placed_hi + placed_lo + placed_hi, axis=1)
        total[...] += lax.dot_general(placed, spread, NT, preferred_element_type=f32)
        return carry

    lax.fori_loop(0, base_ref.shape[0] // GROUP, body, 0)
    for c in range(NVAR):
        lower = total[pl.ds(c * BZ, BZ), 0:PLANES]
        upper = total[pl.ds(c * BZ, BZ), PLANES : 2 * PLANES]
        out_ref[c] = field_ref[c] + (lower + pltpu.roll(upper, 1, axis=0)).T


def push(values, weights, base, field):
    return pl.pallas_call(
        push_kernel,
        out_shape=jax.ShapeDtypeStruct((NVAR, PLANES, BZ), f32),
        in_specs=[pl.BlockSpec(memory_space=pltpu.VMEM)] * 4,
        out_specs=pl.BlockSpec(memory_space=pltpu.VMEM),
        scratch_shapes=[pltpu.VMEM((NVAR * BZ, 2 * PLANES), f32)],
        compiler_params=pltpu.CompilerParams(vmem_limit_bytes=56 * 2**20),
    )(values, weights, base, field.reshape(NVAR, PLANES, BZ))


def exchange(x):
    return lax.all_to_all(x, ("bulk", "valve"), split_axis=0, concat_axis=0, tiled=True)


def body(
    bg_adjoint,
    bg_velocity,
    bg_source,
    bg_iblank,
    valve_adjoint,
    valve_velocity,
    valve_source,
    flux_mix,
    rec_cell,
    donor_base,
    donor_weight,
    slot_count,
):
    weights = exchange(donor_weight[:, 0].transpose(1, 0, 2))
    base = exchange(donor_base[0][:, None, :])
    valve_out, bg_swept = sweep_grids(
        flux_mix, valve_adjoint, valve_velocity, valve_source, bg_adjoint, bg_velocity, bg_source, bg_iblank
    )
    values = exchange(pick(valve_out, rec_cell[0], slot_count))
    bg_out = push(values, weights, base, bg_swept).reshape(bg_adjoint.shape)
    return (bg_out, valve_out)


def solution(mesh):
    placed = (
        P(None, "bulk", "valve", None),
        P(None, "bulk", "valve", None),
        P(None, "bulk", "valve", None),
        P("bulk", "valve", None),
        P(None, "valve", "bulk", None),
        P(None, "valve", "bulk", None),
        P(None, "valve", "bulk", None),
        P(),
        P(("bulk", "valve"), None, None),
        P(("bulk", "valve"), None, None),
        P(None, ("bulk", "valve"), None, None),
        P(("bulk", "valve"), None),
    )
    return jax.shard_map(
        body,
        mesh=mesh,
        in_specs=placed,
        out_specs=(P(None, "bulk", "valve", None), P(None, "valve", "bulk", None)),
        check_vma=False,
    )
```

profile of v0, /device:TPU:0, one launch (start us, length us, event | category | flops | bytes accessed | tf_op | source)
XLA Modules:
  0.0 135.2 jit_solution(7147174046334976607)
XLA Ops:
  0.6 11.1 %all-to-all-start.2 = ((s32[128,1,128]{2,1,0:T(1,128)}), s32[128,1,128]{2,1,0:T(1,128)S(1)}, u32[]{:S(2)}, u32[]{:S(2)}) async-start(s32[128,1,128]{2,1,0:T(1,128)} %bitcast.14), calls=%async_computation.2 | async-start | bytes 131072 | tf_op jit(solution)/shard_map/all_to_all | solution.py:336
  11.8 2.1 %copy.17 = f32[8,1,128,128]{3,0,2,1:T(8,128)} copy(f32[8,1,128,128]{3,2,1,0:T(8,128)} %param.22) | data formatting | bytes 1048576 | tf_op args[10]
  13.9 7.3 %all-to-all-done.2.base_ref = s32[128,1,128]{2,1,0:T(1,128)S(1)} async-done(((s32[128,1,128]{2,1,0:T(1,128)}), s32[128,1,128]{2,1,0:T(1,128)S(1)}, u32[]{:S(2)}, u32[]{:S(2)}) %all-to-all-start.2) | async-done | bytes 65568 | tf_op jit(solution)/shard_map/all_to_all | solution.py:336
  21.2 0.0 copy-start.2
  21.2 0.0 copy-start.3
  21.2 0.6 copy-done.2
  21.8 4.6 %all-to-all-start.1 = ((f32[128,8,128]{2,1,0:T(8,128)}), f32[128,8,128]{2,1,0:T(8,128)S(1)}, u32[]{:S(2)}, u32[]{:S(2)}) async-start(f32[128,8,128]{2,1,0:T(8,128)} %bitcast.9), calls=%async_computation.1 | async-start | bytes 1048576 | tf_op jit(solution)/shard_map/all_to_all | solution.py:336
  26.4 0.0 copy-done.3
  26.5 0.6 copy.14.refs_0_
  27.1 30.4 %shard_map.131 = (f32[5,8,32,128]{3,2,1,0:T(8,128)}, f32[5,8,32,128]{3,2,1,0:T(8,128)}) custom-call(f32[3,5,5]{2,1,0:T(8,128)} %copy.14.refs_0_, f32[5,8,32,128]{3,2,1,0:T(8,128)} %refs_1_.1, f32[3,8,32,128]{3,2,1,0:T(8,128)} %refs_2_.1, f32[5,8,32,128]{3,2,1,0:T(8,128)} %refs_3_.1, f32[5,8,32,128]{3,2,1,0:T(8,128)} %refs_4_.1, f32[3,8,32,128]{3,2,1,0:T(8,128)} %refs_5_.1, ...), custom_call_target="tpu_custom_call" | custom-call | tf_op jit(solution)/shard_map/pallas_call | solution.py:195
  57.5 15.2 %shard_map.132 = f32[128,8,128]{2,1,0:T(8,128)} custom-call(s32[1,128]{1,0:T(1,128)} %count_ref.1, s32[128,1,128]{2,1,0:T(1,128)} %bitcast.13, f32[5,256,128]{2,1,0:T(8,128)} %bitcast.10), custom_call_target="tpu_custom_call" | custom-call | tf_op jit(solution)/shard_map/pallas_call | solution.py:264
  72.7 0.0 all-to-all-done.1.weight_ref
  72.7 0.0 copy-start.1
  72.7 24.8 %all_to_all.15.value_ref = f32[128,8,128]{2,1,0:T(8,128)} all-to-all(f32[128,8,128]{2,1,0:T(8,128)} %shard_map.132), channel_id=1, replica_groups=mesh['bulk'=8,'valve'=16] {'bulk','valve'}, dimensions={0} | all-to-all | bytes 1048576 | tf_op jit(solution)/shard_map/all_to_all | solution.py:336
  97.5 0.0 copy-done.1
  97.5 0.0 copy-start
  97.5 36.8 %shard_map.133 = f32[5,256,128]{2,1,0:T(8,128)} custom-call(f32[128,8,128]{2,1,0:T(8,128)} %all_to_all.15.value_ref, f32[128,8,128]{2,1,0:T(8,128)} %copy-done.1, s32[128,1,128]{2,1,0:T(1,128)} %copy-done.2, f32[5,256,128]{2,1,0:T(8,128)} %bitcast.12), custom_call_target="tpu_custom_call" | custom-call | tf_op jit(solution)/shard_map/pallas_call | solution.py:325
  134.3 0.0 copy-done
  134.3 0.8 copy.19
Async XLA Ops:
  0.6 20.6 %all-to-all-start.2 = ((s32[128,1,128]{2,1,0:T(1,128)}), s32[128,1,128]{2,1,0:T(1,128)S(1)}, u32[]{:S(2)}, u32[]{:S(2)}) async-start(s32[128,1,128]{2,1,0:T(1,128)} %bitcast.14), calls=%async_computation.2 | async-start | bytes 131072 | tf_op jit(solution)/shard_map/all_to_all | solution.py:336
  21.2 0.6 copy-start.2
  21.2 5.3 %copy-start.3 = (f32[3,5,5]{2,0,1:T(4,128)S(1)}, f32[3,5,5]{2,0,1:T(4,128)}, u32[]{:S(2)}) copy-start(f32[3,5,5]{2,0,1:T(4,128)} %param.19) | copy-start | bytes 904
  21.8 50.9 %all-to-all-start.1 = ((f32[128,8,128]{2,1,0:T(8,128)}), f32[128,8,128]{2,1,0:T(8,128)S(1)}, u32[]{:S(2)}, u32[]{:S(2)}) async-start(f32[128,8,128]{2,1,0:T(8,128)} %bitcast.9), calls=%async_computation.1 | async-start | bytes 1048576 | tf_op jit(solution)/shard_map/all_to_all | solution.py:336
  72.7 24.8 %copy-start.1 = (f32[128,8,128]{2,1,0:T(8,128)}, f32[128,8,128]{2,1,0:T(8,128)S(1)}, u32[]{:S(2)}) copy-start(f32[128,8,128]{2,1,0:T(8,128)S(1)} %all-to-all-done.1.weight_ref) | copy-start | bytes 1572868
  97.5 36.8 %copy-start = (f32[5,8,32,128]{3,2,1,0:T(8,128)S(1)}, f32[5,8,32,128]{3,2,1,0:T(8,128)}, u32[]{:S(2)}) copy-start(f32[5,8,32,128]{3,2,1,0:T(8,128)} %get-tuple-element.9) | copy-start | bytes 1966084
where the time goes:
time: 136 us; the launch traced here: 135 us
  Pallas kernels  82.4 us (61%)
  blocking collectives  24.8 us (18%)
  starting transfers between devices  15.8 us (12%)
  waiting for transfers between devices  7.26 us (5%)
  local copies, waits for them, and re-layouts  4.22 us (3%)
    pallas_call x1, Pallas kernels, push(): pl.pallas_call(push_kernel, out_shape=jax.ShapeDtypeStruct((NVAR, PLANES,...  36.8 us
    pallas_call x1, Pallas kernels, sweep_grids(): pl.pallas_call(sweep_kernel, out_shape=(out, out), in_specs=[pl.BlockSpec...  30.4 us
    all_to_all x1, blocking collectives, exchange(): lax.all_to_all(x, ('bulk', 'valve'), split_axis=0, concat_axis=0, tiled=T...  24.8 us
    all_to_all x2, starting transfers between devices, exchange(): lax.all_to_all(x, ('bulk', 'valve'), split_axis=0, concat_axis=0, tiled=T...  15.8 us
    pallas_call x1, Pallas kernels, pick(): pl.pallas_call(pick_kernel, out_shape=jax.ShapeDtypeStruct((owners, 8, CA...  15.2 us
    all_to_all x2, waiting for transfers between devices, exchange(): lax.all_to_all(x, ('bulk', 'valve'), split_axis=0, concat_axis=0, tiled=T...  7.26 us
    unnamed x11, local copies, waits for them, and re-layouts  4.22 us
  transfers between devices with their start and end apart: 2, of which 1 were waited for; matrix products, arithmetic and copies ran while one was open for 2% of the time, Pallas kernels for 34%

commit v1 on v0

--- a/solution.py
+++ b/solution.py
@@ -14,7 +14,7 @@
 BY = 32
 BZ = 128
 PLANES = BX * BY
-GROUP = 16
+PAIRS = BZ // 2
 
 f32 = jnp.float32
 bf16 = jnp.bfloat16
@@ -23,10 +23,31 @@
 MESH = pl.DeviceIdType.MESH
 
 
+def greet_all(bulk, valve):
+    n_bulk, n_valve = lax.axis_size("bulk"), lax.axis_size("valve")
+    owners = n_bulk * n_valve
+    me = bulk * n_valve + valve
+
+    def greet(step, carry):
+        other = lax.rem(me + step, owners)
+        pl.semaphore_signal(
+            pltpu.get_barrier_semaphore(),
+            inc=1,
+            device_id=(other // n_valve, lax.rem(other, n_valve)),
+            device_id_type=MESH,
+        )
+        return carry
+
+    lax.fori_loop(1, owners, greet, 0)
+
+
 def sweep_kernel(*refs):
-    (flux_ref, valve_adj, valve_vel, valve_src, bg_adj, bg_vel, bg_src, bg_blank, valve_out, bg_out) = refs[:10]
-    fields = (refs[10 : 10 + ITERS], refs[10 + ITERS : 10 + 2 * ITERS])
-    (slopes, scale, edge_in, edge_out, load_sem, send_sem, recv_sem) = refs[10 + 2 * ITERS :]
+    (flux_ref, valve_adj, valve_vel, valve_src, bg_adj, bg_vel, bg_src, bg_blank) = refs[:8]
+    (weight_ref, base_ref, valve_out, bg_out, donors_in) = refs[8:13]
+    fields = (refs[13 : 13 + ITERS], refs[13 + ITERS : 13 + 2 * ITERS])
+    (slopes, scale, edge_in, edge_out, donors_out, load_sem, send_sem, recv_sem, away_sem, home_sem, own_sem) = refs[
+        13 + 2 * ITERS :
+    ]
     bulk, valve = lax.axis_index("bulk"), lax.axis_index("valve")
     n_bulk, n_valve = lax.axis_size("bulk"), lax.axis_size("valve")
     place = {"bulk": (bulk, n_bulk), "valve": (valve, n_valve)}
@@ -60,13 +81,7 @@
         for side in range(2):
             clear(g, side)
 
-    barrier = pltpu.get_barrier_semaphore()
-    for axis in ("bulk", "valve"):
-        index, count = place[axis]
-        for step in (1, count - 1):
-            pl.semaphore_signal(
-                barrier, inc=1, device_id={axis: lax.rem(index + step, count)}, device_id_type=MESH
-            )
+    greet_all(bulk, valve)
 
     def slope_rows(x, carry):
         for g in range(2):
@@ -169,48 +184,94 @@
 
         lax.fori_loop(0, BX, rows, 0)
 
+    owners = n_bulk * n_valve
+    for k in range(7):
+        donors_out[pl.ds(k, owners, stride=8), :] = weight_ref[k]
+    donors_out[pl.ds(7, owners, stride=8), :] = base_ref[...].astype(f32)
+    me = bulk * n_valve + valve
+
+    def donor_copy(owner, landing):
+        return pltpu.make_async_remote_copy(
+            src_ref=donors_out.at[pl.ds(pl.multiple_of(owner * 8, 8), 8)],
+            dst_ref=donors_in.at[landing],
+            send_sem=away_sem.at[owner],
+            recv_sem=home_sem.at[landing],
+            device_id=(owner // n_valve, lax.rem(owner, n_valve)),
+            device_id_type=MESH,
+        )
+
+    def send_donors(part):
+        first = lax.rem(bulk + part, n_bulk) * n_valve
+
+        def one(v, carry):
+            owner = first + lax.rem(valve + v, n_valve)
+            pl.when(owner != me)(donor_copy(owner, me).start)
+            return carry
+
+        lax.fori_loop(0, n_valve, one, 0)
+
+    own = pltpu.make_async_copy(
+        donors_out.at[pl.ds(pl.multiple_of(me * 8, 8), 8)], donors_in.at[me], own_sem
+    )
+    own.start()
     for g in range(2):
         loads[g].wait()
         first_edges(g)
-    pl.semaphore_wait(barrier, 4)
+    lax.fori_loop(0, BX, slope_rows, 0)
+    pl.semaphore_wait(pltpu.get_barrier_semaphore(), owners - 1)
     for g in range(2):
         send(g, 0)
-    lax.fori_loop(0, BX, slope_rows, 0)
+    part = 0
     for t in range(ITERS):
         for g in range(2):
+            while part * 2 * ITERS < n_bulk * (t * 2 + g + 1):
+                send_donors(part)
+                part += 1
             arrive(g, t)
             sweep(g, t)
             if t + 1 < ITERS:
                 send(g, t + 1)
+    own.wait()
+
+    def settle(owner, carry):
+        pl.when(owner != me)(donor_copy(owner, owner).wait)
+        return carry
+
+    lax.fori_loop(0, owners, settle, 0)
     for t in range(ITERS):
         for g in range(2):
             left(g, t)
 
 
-def sweep_grids(flux_mix, valve_adj, valve_vel, valve_src, bg_adj, bg_vel, bg_src, bg_blank):
+def sweep_grids(flux_mix, valve_adj, valve_vel, valve_src, bg_adj, bg_vel, bg_src, bg_blank, weights, base):
     whole = pl.BlockSpec(memory_space=pltpu.VMEM)
     far = pl.BlockSpec(memory_space=pl.ANY)
+    owners = base.shape[0]
     out = jax.ShapeDtypeStruct(valve_adj.shape, f32)
     edges = pltpu.VMEM((2, ITERS, 2, NVAR, BX, 1, BZ), f32)
     return pl.pallas_call(
         sweep_kernel,
-        out_shape=(out, out),
-        in_specs=[pl.BlockSpec(memory_space=pltpu.SMEM), far, whole, whole, far, whole, whole, whole],
-        out_specs=(whole, whole),
+        out_shape=(out, out, jax.ShapeDtypeStruct((owners, 8, CAP), f32)),
+        in_specs=[pl.BlockSpec(memory_space=pltpu.SMEM), far, whole, whole, far, whole, whole, whole, whole, whole],
+        out_specs=(whole, whole, far),
         scratch_shapes=[pltpu.VMEM((NVAR, BX + 2, BY, BZ), f32)] * (2 * ITERS)
         + [
             pltpu.VMEM((2, 3, BX, BY, BZ), f32),
             pltpu.VMEM((BX, BY, BZ), f32),
             edges,
             edges,
+            pltpu.VMEM((owners * 8, CAP), f32),
             pltpu.SemaphoreType.DMA((2,)),
             pltpu.SemaphoreType.DMA((2, ITERS, 2, 2)),
             pltpu.SemaphoreType.DMA((2, ITERS, 2, 2)),
+            pltpu.SemaphoreType.DMA((owners,)),
+            pltpu.SemaphoreType.DMA((owners,)),
+            pltpu.SemaphoreType.DMA,
         ],
         compiler_params=pltpu.CompilerParams(
             collective_id=0, has_side_effects=True, vmem_limit_bytes=56 * 2**20
         ),
-    )(flux_mix, valve_adj, valve_vel, valve_src, bg_adj, bg_vel, bg_src, bg_blank)
+    )(flux_mix, valve_adj, valve_vel, valve_src, bg_adj, bg_vel, bg_src, bg_blank, weights, base)
 
 
 def split(x):
@@ -222,28 +283,48 @@
     return x.astype(f32).astype(bf16)
 
 
-def pick_kernel(count_ref, cell_ref, field_ref, out_ref, table):
+def donor_kernel(
+    count_ref, cell_ref, field_ref, donor_ref, swept_ref, out_ref, table, picked, arrived, total, mixed, away_sem, home_sem
+):
+    bulk, valve = lax.axis_index("bulk"), lax.axis_index("valve")
+    n_bulk, n_valve = lax.axis_size("bulk"), lax.axis_size("valve")
+    owners = n_bulk * n_valve
+    me = bulk * n_valve + valve
+    greet_all(bulk, valve)
+
     for c in range(NVAR):
         hi, lo = split(field_ref[c].T)
         table[pl.ds(c * BZ, BZ), 0:PLANES] = hi
         table[pl.ds(c * BZ, BZ), PLANES : 2 * PLANES] = lo
+    total[...] = jnp.zeros_like(total)
     plane_row = as_bf16(lax.broadcasted_iota(jnp.int32, (PLANES, CAP), 0))
     depth_row = lax.broadcasted_iota(jnp.int32, (BZ, CAP), 0)
+    pair_row = as_bf16(lax.broadcasted_iota(jnp.int32, (PAIRS, CAP), 0))
     slot = lax.broadcasted_iota(jnp.int32, (1, CAP), 1)
     one, zero = jnp.ones((), bf16), jnp.zeros((), bf16)
 
-    def body(block, carry):
+    def value_copy(owner, landing):
+        return pltpu.make_async_remote_copy(
+            src_ref=picked.at[owner],
+            dst_ref=arrived.at[landing],
+            send_sem=away_sem.at[owner],
+            recv_sem=home_sem.at[landing],
+            device_id=(owner // n_valve, lax.rem(owner, n_valve)),
+            device_id_type=MESH,
+        )
+
+    def pick(part, carry):
+        first = lax.rem(bulk + part, n_bulk) * n_valve
         hits, depths = [], []
-        for u in range(GROUP):
-            owner = block * GROUP + u
-            cell = cell_ref[owner]
+        for u in range(n_valve):
+            cell = cell_ref[first + u]
             hits.append(jnp.where(plane_row == as_bf16(cell >> 7), one, zero))
-            depths.append(jnp.where(slot < count_ref[0, owner], cell & (BZ - 1), -1))
+            depths.append(jnp.where(slot < count_ref[0, first + u], cell & (BZ - 1), -1))
         hits = jnp.concatenate(hits, axis=1)
         columns = lax.dot_general(
             table[...], jnp.concatenate([hits, hits], axis=0), NN, preferred_element_type=f32
         )
-        for u in range(GROUP):
+        for u in range(n_valve):
             here = depth_row == depths[u]
             rows = [
                 jnp.sum(
@@ -253,51 +334,46 @@
                 )
                 for c in range(NVAR)
             ]
-            out_ref[block * GROUP + u] = jnp.concatenate(rows + [jnp.zeros((3, CAP), f32)], axis=0)
-        return carry
-
-    lax.fori_loop(0, out_ref.shape[0] // GROUP, body, 0)
-
-
-def pick(field, cells, counts):
-    owners = cells.shape[0]
-    return pl.pallas_call(
-        pick_kernel,
-        out_shape=jax.ShapeDtypeStruct((owners, 8, CAP), f32),
-        in_specs=[
-            pl.BlockSpec(memory_space=pltpu.SMEM),
-            pl.BlockSpec(memory_space=pltpu.VMEM),
-            pl.BlockSpec(memory_space=pltpu.VMEM),
-        ],
-        out_specs=pl.BlockSpec(memory_space=pltpu.VMEM),
-        scratch_shapes=[pltpu.VMEM((NVAR * BZ, 2 * PLANES), bf16)],
-        compiler_params=pltpu.CompilerParams(vmem_limit_bytes=56 * 2**20),
-    )(counts, cells.reshape(owners, 1, CAP), field.reshape(NVAR, PLANES, BZ))
-
-
-def push_kernel(value_ref, weight_ref, base_ref, field_ref, out_ref, total):
-    total[...] = jnp.zeros_like(total)
-    plane_row = as_bf16(lax.broadcasted_iota(jnp.int32, (PLANES, CAP), 0))
-    depth_row = as_bf16(lax.broadcasted_iota(jnp.int32, (BZ, CAP), 0))
-    zero = jnp.zeros((), bf16)
+            picked[first + u] = jnp.concatenate(rows, axis=0)
+
+        @pl.when(part == 0)
+        def _():
+            pl.semaphore_wait(pltpu.get_barrier_semaphore(), owners - 1)
+            arrived[me] = picked[me]
+
+        def send(v, carry):
+            owner = first + lax.rem(valve + v, n_valve)
+            pl.when(owner != me)(value_copy(owner, me).start)
+            return carry
+
+        return lax.fori_loop(0, n_valve, send, carry)
+
+    lax.fori_loop(0, n_bulk, pick, 0)
 
     def terms(sender):
-        base = base_ref[sender]
+        base = donor_ref[sender, 7:8].astype(jnp.int32)
         plane = base >> 7
-        weight_hi, weight_lo = split(weight_ref[sender])
-        value_hi, value_lo = split(value_ref[sender])
+        odd = (base & 1) == 1
+        weight = [donor_ref[sender, k : k + 1] for k in range(7)]
+        weight.append(1.0 - ((weight[0] + weight[1]) + (weight[2] + weight[3]) + (weight[4] + weight[5]) + weight[6]))
+        rows = []
+        for pair in range(4):
+            near, deep = weight[2 * pair], weight[2 * pair + 1]
+            rows += [jnp.where(odd, 0.0, near), jnp.where(odd, near, deep), jnp.where(odd, deep, 0.0)]
+        weight_hi, weight_lo = split(jnp.concatenate(rows, axis=0))
+        value_hi, value_lo = split(arrived[sender])
         hits = [plane_row == as_bf16(plane + off) for off in (0, 1, BY, BY + 1)]
 
         def spread(weight):
-            halves = []
-            for step in range(2):
+            thirds = []
+            for step in range(3):
                 rows = jnp.zeros((PLANES, CAP), bf16)
                 for pair in range(4):
-                    rows = jnp.where(hits[pair], weight[2 * pair + step : 2 * pair + step + 1], rows)
-                halves.append(rows)
-            return jnp.concatenate(halves, axis=0)
-
-        here = depth_row == as_bf16(base & (BZ - 1))
+                    rows = jnp.where(hits[pair], weight[3 * pair + step : 3 * pair + step + 1], rows)
+                thirds.append(rows)
+            return jnp.concatenate(thirds, axis=0)
+
+        here = pair_row == as_bf16((base & (BZ - 1)) >> 1)
 
         def placed(value):
             return jnp.concatenate(
@@ -306,34 +382,71 @@
 
         return spread(weight_hi), spread(weight_lo), placed(value_hi), placed(value_lo)
 
-    def body(block, carry):
-        parts = [terms(block * GROUP + u) for u in range(GROUP)]
-        spread_hi, spread_lo, placed_hi, placed_lo = [[part[i] for part in parts] for i in range(4)]
-        spread = jnp.concatenate(spread_hi + spread_hi + spread_lo, axis=1)
-        placed = jnp.concatenate(placed_hi + placed_lo + placed_hi, axis=1)
-        total[...] += lax.dot_general(placed, spread, NT, preferred_element_type=f32)
+    def push(part, carry):
+        first = lax.rem(bulk - part + n_bulk, n_bulk) * n_valve
+
+        def land(v, carry):
+            sender = first + v
+            pl.when(sender != me)(value_copy(sender, sender).wait_recv)
+            return carry
+
+        lax.fori_loop(0, n_valve, land, 0)
+        parts = [terms(first + u) for u in range(n_valve)]
+        spread_hi, spread_lo, placed_hi, placed_lo = [
+            jnp.concatenate([part[i] for part in parts], axis=1) for i in range(4)
+        ]
+        both = lax.dot_general(
+            jnp.concatenate([placed_hi, placed_lo], axis=0), spread_hi, NT, preferred_element_type=f32
+        )
+        low = lax.dot_general(placed_hi, spread_lo, NT, preferred_element_type=f32)
+        total[...] += both[: NVAR * PAIRS] + both[NVAR * PAIRS :] + low
         return carry
 
-    lax.fori_loop(0, base_ref.shape[0] // GROUP, body, 0)
+    lax.fori_loop(0, n_bulk, push, 0)
     for c in range(NVAR):
-        lower = total[pl.ds(c * BZ, BZ), 0:PLANES]
-        upper = total[pl.ds(c * BZ, BZ), PLANES : 2 * PLANES]
-        out_ref[c] = field_ref[c] + (lower + pltpu.roll(upper, 1, axis=0)).T
-
-
-def push(values, weights, base, field):
+        rows = pl.ds(c * PAIRS, PAIRS)
+        even = total[rows, 0:PLANES] + pltpu.roll(total[rows, 2 * PLANES : 3 * PLANES], 1, axis=0)
+        odd = total[rows, PLANES : 2 * PLANES]
+        for half in range(PLANES // BZ):
+            columns = slice(half * BZ, (half + 1) * BZ)
+            mixed[half, pl.ds(0, PAIRS, stride=2), :] = even[:, columns]
+            mixed[half, pl.ds(1, PAIRS, stride=2), :] = odd[:, columns]
+            out_ref[c, pl.ds(half * BZ, BZ), :] = swept_ref[c, pl.ds(half * BZ, BZ), :] + mixed[half].T
+
+    def left(owner, carry):
+        pl.when(owner != me)(value_copy(owner, me).wait_send)
+        return carry
+
+    lax.fori_loop(0, owners, left, 0)
+
+
+def donor_terms(field, cells, counts, donors, swept):
+    owners = cells.shape[0]
+    whole = pl.BlockSpec(memory_space=pltpu.VMEM)
     return pl.pallas_call(
-        push_kernel,
+        donor_kernel,
         out_shape=jax.ShapeDtypeStruct((NVAR, PLANES, BZ), f32),
-        in_specs=[pl.BlockSpec(memory_space=pltpu.VMEM)] * 4,
-        out_specs=pl.BlockSpec(memory_space=pltpu.VMEM),
-        scratch_shapes=[pltpu.VMEM((NVAR * BZ, 2 * PLANES), f32)],
-        compiler_params=pltpu.CompilerParams(vmem_limit_bytes=56 * 2**20),
-    )(values, weights, base, field.reshape(NVAR, PLANES, BZ))
-
-
-def exchange(x):
-    return lax.all_to_all(x, ("bulk", "valve"), split_axis=0, concat_axis=0, tiled=True)
+        in_specs=[pl.BlockSpec(memory_space=pltpu.SMEM)] + [whole] * 4,
+        out_specs=whole,
+        scratch_shapes=[
+            pltpu.VMEM((NVAR * BZ, 2 * PLANES), bf16),
+            pltpu.VMEM((owners, NVAR, CAP), f32),
+            pltpu.VMEM((owners, NVAR, CAP), f32),
+            pltpu.VMEM((NVAR * PAIRS, 3 * PLANES), f32),
+            pltpu.VMEM((PLANES // BZ, BZ, BZ), f32),
+            pltpu.SemaphoreType.DMA((owners,)),
+            pltpu.SemaphoreType.DMA((owners,)),
+        ],
+        compiler_params=pltpu.CompilerParams(
+            collective_id=1, has_side_effects=True, vmem_limit_bytes=56 * 2**20
+        ),
+    )(
+        counts,
+        cells.reshape(owners, 1, CAP),
+        field.reshape(NVAR, PLANES, BZ),
+        donors,
+        swept.reshape(NVAR, PLANES, BZ),
+    )
 
 
 def body(
@@ -350,13 +463,19 @@
     donor_weight,
     slot_count,
 ):
-    weights = exchange(donor_weight[:, 0].transpose(1, 0, 2))
-    base = exchange(donor_base[0][:, None, :])
-    valve_out, bg_swept = sweep_grids(
-        flux_mix, valve_adjoint, valve_velocity, valve_source, bg_adjoint, bg_velocity, bg_source, bg_iblank
+    valve_out, bg_swept, donors = sweep_grids(
+        flux_mix,
+        valve_adjoint,
+        valve_velocity,
+        valve_source,
+        bg_adjoint,
+        bg_velocity,
+        bg_source,
+        bg_iblank,
+        donor_weight[:, 0],
+        donor_base[0],
     )
-    values = exchange(pick(valve_out, rec_cell[0], slot_count))
-    bg_out = push(values, weights, base, bg_swept).reshape(bg_adjoint.shape)
+    bg_out = donor_terms(valve_out, rec_cell[0], slot_count, donors, bg_swept).reshape(bg_adjoint.shape)
     return (bg_out, valve_out)
 
 

time: 136 us -> 108 us (0.79)
  blocking collectives: 24.8 us -> 0 us
  Pallas kernels: 82.4 us -> 102 us
  starting transfers between devices: 15.8 us -> 0 us
  waiting for transfers between devices: 7.26 us -> 0 us
    all_to_all x1 -> x0, blocking collectives: 24.8 us -> none  [exchange(): lax.all_to_all(x, ('bulk', 'valve'), split_axis=0, concat_axis=0, tiled=T...]
    pallas_call x3 -> x2, Pallas kernels: 82.4 us -> 102 us  [the longest x1 57.2 us: donor_terms(): pl.pallas_call(donor_kernel, out_shape=jax.ShapeDtypeStruct((NVAR, PLANES...]
    all_to_all x2 -> x0, starting transfers between devices: 15.8 us -> none  [exchange(): lax.all_to_all(x, ('bulk', 'valve'), split_axis=0, concat_axis=0, tiled=T...]
    all_to_all x2 -> x0, waiting for transfers between devices: 7.26 us -> none  [exchange(): lax.all_to_all(x, ('bulk', 'valve'), split_axis=0, concat_axis=0, tiled=T...]
    unnamed x11 -> x5, local copies, waits for them, and re-layouts: 4.22 us -> 4.2 us
  transfers between devices with their start and end apart: 2 -> 0, of which waited for: 1 -> 0; matrix products, arithmetic and copies ran while one was open for 2% -> 0% of each run, Pallas kernels for 34% -> 0%
where the time goes in v1:
time: 108 us; the launch traced here: 107 us
  Pallas kernels  102 us (94%)
  local copies, waits for them, and re-layouts  4.2 us (4%)
    pallas_call x1, Pallas kernels, donor_terms(): pl.pallas_call(donor_kernel, out_shape=jax.ShapeDtypeStruct((NVAR, PLANES...  57.2 us
    pallas_call x1, Pallas kernels, sweep_grids(): pl.pallas_call(sweep_kernel, out_shape=(out, out, jax.ShapeDtypeStruct((o...  44.8 us
    unnamed x5, local copies, waits for them, and re-layouts  4.2 us

profile of v1, /device:TPU:0, one launch (start us, length us, event | category | flops | bytes accessed | tf_op | source)
XLA Modules:
  0.0 106.8 jit_solution(5547358194180560961)
XLA Ops:
  0.6 1.3 %copy.14.refs_0_ = f32[3,5,5]{2,1,0:T(8,128)} copy(f32[3,5,5]{2,0,1:T(4,128)} %param.19) | data formatting | bytes 600 | tf_op args[7]
  1.9 44.8 %shard_map.131 = (f32[5,8,32,128]{3,2,1,0:T(8,128)}, f32[5,8,32,128]{3,2,1,0:T(8,128)}, f32[128,8,128]{2,1,0:T(8,128)}) custom-call(f32[3,5,5]{2,1,0:T(8,128)} %copy.14.refs_0_, f32[5,8,32,128]{3,2,1,0:T(8,128)} %refs_1_.1, f32[3,8,32,128]{3,2,1,0:T(8,128)} %refs_2_.1, f32[5,8,32,128]{3,2,1,0:T(8,128)} %refs_3_.1, f32[5,8,32,128]{3,2,1,0:T(8,128)} %refs_4_.1, ...), custom_call_target="tpu_custom_call" | custom-call | tf_op jit(solution)/shard_map/pallas_call | solution.py:252
  46.7 57.2 %shard_map.132 = f32[5,256,128]{2,1,0:T(8,128)} custom-call(s32[1,128]{1,0:T(1,128)} %count_ref.1, s32[128,1,128]{2,1,0:T(1,128)} %bitcast.11, f32[5,256,128]{2,1,0:T(8,128)} %bitcast.6, f32[128,8,128]{2,1,0:T(8,128)} %get-tuple-element.6.donor_ref, f32[5,256,128]{2,1,0:T(8,128)} %bitcast.8), custom_call_target="tpu_custom_call" | custom-call | tf_op jit(solution)/shard_map/pallas_call | solution.py:426
  103.9 0.0 copy-start
  103.9 2.1 %copy.17 = f32[5,8,32,128]{3,2,1,0:T(8,128)} copy(f32[5,8,32,128]{3,2,1,0:T(8,128)} %bitcast.7) | data formatting | bytes 1310720
  106.0 0.0 copy-done
  106.0 0.8 copy.18
Async XLA Ops:
  103.9 2.1 %copy-start = (f32[5,8,32,128]{3,2,1,0:T(8,128)S(1)}, f32[5,8,32,128]{3,2,1,0:T(8,128)}, u32[]{:S(2)}) copy-start(f32[5,8,32,128]{3,2,1,0:T(8,128)} %get-tuple-element.11) | copy-start | bytes 1966084

commit v2 on v1

--- a/solution.py
+++ b/solution.py
@@ -15,6 +15,7 @@
 BZ = 128
 PLANES = BX * BY
 PAIRS = BZ // 2
+ROWS = 2
 
 f32 = jnp.float32
 bf16 = jnp.bfloat16
@@ -23,31 +24,89 @@
 MESH = pl.DeviceIdType.MESH
 
 
-def greet_all(bulk, valve):
+def greet(bulk, valve):
     n_bulk, n_valve = lax.axis_size("bulk"), lax.axis_size("valve")
-    owners = n_bulk * n_valve
-    me = bulk * n_valve + valve
-
-    def greet(step, carry):
-        other = lax.rem(me + step, owners)
-        pl.semaphore_signal(
-            pltpu.get_barrier_semaphore(),
-            inc=1,
-            device_id=(other // n_valve, lax.rem(other, n_valve)),
+    barrier = pltpu.get_barrier_semaphore()
+    for step in range(1, n_bulk):
+        other = (lax.rem(bulk + step, n_bulk), valve)
+        pl.semaphore_signal(barrier, inc=1, device_id=other, device_id_type=MESH)
+    for step in range(1, n_valve):
+        other = (bulk, lax.rem(valve + step, n_valve))
+        pl.semaphore_signal(barrier, inc=1, device_id=other, device_id_type=MESH)
+
+
+def greeted():
+    pl.semaphore_wait(pltpu.get_barrier_semaphore(), lax.axis_size("bulk") + lax.axis_size("valve") - 2)
+
+
+class Exchange:
+    def __init__(self, source, middle, block, landed, sems):
+        self.bulk, self.valve = lax.axis_index("bulk"), lax.axis_index("valve")
+        self.n_bulk, self.n_valve = lax.axis_size("bulk"), lax.axis_size("valve")
+        self.source, self.middle, self.block, self.landed = source, middle, block, landed
+        self.sems = sems
+
+    def first(self, v, landing):
+        return pltpu.make_async_remote_copy(
+            src_ref=self.source(v),
+            dst_ref=self.middle.at[landing],
+            send_sem=self.sems[0].at[v],
+            recv_sem=self.sems[1].at[landing],
+            device_id=(self.bulk, v),
             device_id_type=MESH,
         )
-        return carry
-
-    lax.fori_loop(1, owners, greet, 0)
+
+    def second(self, b, landing):
+        return pltpu.make_async_remote_copy(
+            src_ref=self.block(b),
+            dst_ref=self.landed.at[landing],
+            send_sem=self.sems[2].at[b],
+            recv_sem=self.sems[3].at[landing],
+            device_id=(b, self.valve),
+            device_id_type=MESH,
+        )
+
+    def start_first(self, step):
+        self.first(lax.rem(self.valve + step, self.n_valve), self.valve).start()
+
+    def finish_first(self):
+        for step in range(1, self.n_valve):
+            v = lax.rem(self.valve + step, self.n_valve)
+            self.first(v, v).wait_recv()
+
+    def start_second(self):
+        for step in range(1, self.n_bulk):
+            self.second(lax.rem(self.bulk + step, self.n_bulk), self.bulk).start()
+
+    def finish_second(self, b):
+        self.second(b, b).wait_recv()
+
+    def sent(self):
+        for step in range(1, self.n_valve):
+            v = lax.rem(self.valve + step, self.n_valve)
+            self.first(v, v).wait_send()
+        for step in range(1, self.n_bulk):
+            b = lax.rem(self.bulk + step, self.n_bulk)
+            self.second(b, b).wait_send()
+
+
+def exchange_sems(n_bulk, n_valve):
+    return [
+        pltpu.SemaphoreType.DMA((n_valve,)),
+        pltpu.SemaphoreType.DMA((n_valve,)),
+        pltpu.SemaphoreType.DMA((n_bulk,)),
+        pltpu.SemaphoreType.DMA((n_bulk,)),
+    ]
 
 
 def sweep_kernel(*refs):
     (flux_ref, valve_adj, valve_vel, valve_src, bg_adj, bg_vel, bg_src, bg_blank) = refs[:8]
     (weight_ref, base_ref, valve_out, bg_out, donors_in) = refs[8:13]
     fields = (refs[13 : 13 + ITERS], refs[13 + ITERS : 13 + 2 * ITERS])
-    (slopes, scale, edge_in, edge_out, donors_out, load_sem, send_sem, recv_sem, away_sem, home_sem, own_sem) = refs[
-        13 + 2 * ITERS :
+    (slopes, scale, edge_in, edge_out, mix, donors_out, donors_mid, load_sem, send_sem, recv_sem, own_sem) = refs[
+        13 + 2 * ITERS : 24 + 2 * ITERS
     ]
+    donor_sems = refs[24 + 2 * ITERS :]
     bulk, valve = lax.axis_index("bulk"), lax.axis_index("valve")
     n_bulk, n_valve = lax.axis_size("bulk"), lax.axis_size("valve")
     place = {"bulk": (bulk, n_bulk), "valve": (valve, n_valve)}
@@ -81,7 +140,7 @@
         for side in range(2):
             clear(g, side)
 
-    greet_all(bulk, valve)
+    greet(bulk, valve)
 
     def slope_rows(x, carry):
         for g in range(2):
@@ -121,10 +180,10 @@
             )
         return found
 
-    def send(g, t):
+    def send(g, t, kind):
         for side in range(2):
-            for sends, _, copy in copies(g, t, side):
-                pl.when(sends)(copy.start)
+            sends, _, copy = copies(g, t, side)[kind]
+            pl.when(sends)(copy.start)
 
     def arrive(g, t):
         for side in range(2):
@@ -138,6 +197,9 @@
 
     row = lax.broadcasted_iota(jnp.int32, (BY, BZ), 0)
     lane = lax.broadcasted_iota(jnp.int32, (BY, BZ), 1)
+
+    def fold(x):
+        return x.reshape(BY // 8, 8, BZ)
 
     def sweep(g, t):
         now = fields[g][t]
@@ -153,17 +215,17 @@
                 z_low = jnp.where(lane == 0, 0.0, pltpu.roll(here, 1, axis=1))
                 z_high = jnp.where(lane == BZ - 1, 0.0, pltpu.roll(here, BZ - 1, axis=1))
                 around.append(
-                    (x_low + x_high) + (y_low + y_high) + (z_low + z_high) + source[c, x]
+                    fold((x_low + x_high) + (y_low + y_high) + (z_low + z_high) + source[c, x])
                 )
                 for d, (low, high) in enumerate(((x_low, x_high), (y_low, y_high), (z_low, z_high))):
-                    steep[d].append(slopes[g, d, x] * (low - high))
+                    steep[d].append(fold(slopes[g, d, x] * (low - high)))
             factor = scale[x] if g else 1.0 / 12.0
             for i in range(NVAR):
                 total = around[i]
                 for d in range(3):
                     for j in range(NVAR):
-                        total = total - flux_ref[d, j, i] * steep[d][j]
-                total = total * factor
+                        total = total - mix[(d * NVAR + j) * NVAR + i] * steep[d][j]
+                total = total.reshape(BY, BZ) * factor
                 if t == ITERS - 1:
                     outputs[g][i, x] = total
                 else:
@@ -172,7 +234,12 @@
                     edge_out[g, t + 1, 1, i, x] = total[BY - 1 : BY]
             return carry
 
-        lax.fori_loop(0, BX, rows, 0)
+        lax.fori_loop(0, 2, lambda k, carry: rows(k * (BX - 1), carry), 0, unroll=2)
+        if t + 1 < ITERS:
+            send(g, t + 1, 0)
+        lax.fori_loop(1, BX - 1, rows, 0, unroll=2)
+        if t + 1 < ITERS:
+            send(g, t + 1, 1)
 
     def first_edges(g):
         def rows(x, carry):
@@ -184,60 +251,50 @@
 
         lax.fori_loop(0, BX, rows, 0)
 
-    owners = n_bulk * n_valve
-    for k in range(7):
-        donors_out[pl.ds(k, owners, stride=8), :] = weight_ref[k]
-    donors_out[pl.ds(7, owners, stride=8), :] = base_ref[...].astype(f32)
-    me = bulk * n_valve + valve
-
-    def donor_copy(owner, landing):
-        return pltpu.make_async_remote_copy(
-            src_ref=donors_out.at[pl.ds(pl.multiple_of(owner * 8, 8), 8)],
-            dst_ref=donors_in.at[landing],
-            send_sem=away_sem.at[owner],
-            recv_sem=home_sem.at[landing],
-            device_id=(owner // n_valve, lax.rem(owner, n_valve)),
-            device_id_type=MESH,
-        )
-
-    def send_donors(part):
-        first = lax.rem(bulk + part, n_bulk) * n_valve
-
-        def one(v, carry):
-            owner = first + lax.rem(valve + v, n_valve)
-            pl.when(owner != me)(donor_copy(owner, me).start)
-            return carry
-
-        lax.fori_loop(0, n_valve, one, 0)
-
-    own = pltpu.make_async_copy(
-        donors_out.at[pl.ds(pl.multiple_of(me * 8, 8), 8)], donors_in.at[me], own_sem
+    for b in range(n_bulk):
+        owners = pl.ds(b * n_valve, n_valve)
+        for k in range(7):
+            donors_out[pl.ds(b * 8 + k, n_valve, stride=n_bulk * 8), :] = weight_ref[k, owners]
+        donors_out[pl.ds(b * 8 + 7, n_valve, stride=n_bulk * 8), :] = base_ref[owners].astype(f32)
+
+    def aligned(index, size):
+        return pl.ds(pl.multiple_of(index * size, size), size)
+
+    donors = Exchange(
+        lambda v: donors_out.at[aligned(v, n_bulk * 8)],
+        donors_mid,
+        lambda b: donors_mid.at[:, aligned(b, 8)],
+        donors_in,
+        donor_sems,
     )
-    own.start()
     for g in range(2):
         loads[g].wait()
         first_edges(g)
+    greeted()
+    for g in range(2):
+        for kind in range(2):
+            send(g, 0, kind)
+    for step in range(1, n_valve):
+        donors.start_first(step)
+    donors_mid[valve] = donors_out[aligned(valve, n_bulk * 8)]
     lax.fori_loop(0, BX, slope_rows, 0)
-    pl.semaphore_wait(pltpu.get_barrier_semaphore(), owners - 1)
-    for g in range(2):
-        send(g, 0)
-    part = 0
+    for d in range(3):
+        for j in range(NVAR):
+            for i in range(NVAR):
+                mix[(d * NVAR + j) * NVAR + i] = jnp.broadcast_to(flux_ref[d, j : j + 1, i : i + 1], (8, BZ))
+    own = pltpu.make_async_copy(donors.block(bulk), donors_in.at[bulk], own_sem)
     for t in range(ITERS):
         for g in range(2):
-            while part * 2 * ITERS < n_bulk * (t * 2 + g + 1):
-                send_donors(part)
-                part += 1
             arrive(g, t)
             sweep(g, t)
-            if t + 1 < ITERS:
-                send(g, t + 1)
+        if t == 1:
+            donors.finish_first()
+            donors.start_second()
+            own.start()
     own.wait()
-
-    def settle(owner, carry):
-        pl.when(owner != me)(donor_copy(owner, owner).wait)
-        return carry
-
-    lax.fori_loop(0, owners, settle, 0)
+    for step in range(1, n_bulk):
+        donors.finish_second(lax.rem(bulk + step, n_bulk))
+    donors.sent()
     for t in range(ITERS):
         for g in range(2):
             left(g, t)
@@ -246,13 +303,13 @@
 def sweep_grids(flux_mix, valve_adj, valve_vel, valve_src, bg_adj, bg_vel, bg_src, bg_blank, weights, base):
     whole = pl.BlockSpec(memory_space=pltpu.VMEM)
     far = pl.BlockSpec(memory_space=pl.ANY)
-    owners = base.shape[0]
+    n_bulk, n_valve = lax.axis_size("bulk"), lax.axis_size("valve")
     out = jax.ShapeDtypeStruct(valve_adj.shape, f32)
     edges = pltpu.VMEM((2, ITERS, 2, NVAR, BX, 1, BZ), f32)
     return pl.pallas_call(
         sweep_kernel,
-        out_shape=(out, out, jax.ShapeDtypeStruct((owners, 8, CAP), f32)),
-        in_specs=[pl.BlockSpec(memory_space=pltpu.SMEM), far, whole, whole, far, whole, whole, whole, whole, whole],
+        out_shape=(out, out, jax.ShapeDtypeStruct((n_bulk, n_valve, 8, CAP), f32)),
+        in_specs=[whole, far, whole, whole, far, whole, whole, whole, whole, whole],
         out_specs=(whole, whole, far),
         scratch_shapes=[pltpu.VMEM((NVAR, BX + 2, BY, BZ), f32)] * (2 * ITERS)
         + [
@@ -260,14 +317,15 @@
             pltpu.VMEM((BX, BY, BZ), f32),
             edges,
             edges,
-            pltpu.VMEM((owners * 8, CAP), f32),
+            pltpu.VMEM((3 * NVAR * NVAR, 8, BZ), f32),
+            pltpu.VMEM((n_valve * n_bulk * 8, CAP), f32),
+            pltpu.VMEM((n_valve, n_bulk * 8, CAP), f32),
             pltpu.SemaphoreType.DMA((2,)),
             pltpu.SemaphoreType.DMA((2, ITERS, 2, 2)),
             pltpu.SemaphoreType.DMA((2, ITERS, 2, 2)),
-            pltpu.SemaphoreType.DMA((owners,)),
-            pltpu.SemaphoreType.DMA((owners,)),
             pltpu.SemaphoreType.DMA,
-        ],
+        ]
+        + exchange_sems(n_bulk, n_valve),
         compiler_params=pltpu.CompilerParams(
             collective_id=0, has_side_effects=True, vmem_limit_bytes=56 * 2**20
         ),
@@ -284,13 +342,11 @@
 
 
 def donor_kernel(
-    count_ref, cell_ref, field_ref, donor_ref, swept_ref, out_ref, table, picked, arrived, total, mixed, away_sem, home_sem
+    count_ref, cell_ref, field_ref, donor_ref, out_ref, table, picked, middle, arrived, total, mixed, *value_sems
 ):
     bulk, valve = lax.axis_index("bulk"), lax.axis_index("valve")
     n_bulk, n_valve = lax.axis_size("bulk"), lax.axis_size("valve")
-    owners = n_bulk * n_valve
-    me = bulk * n_valve + valve
-    greet_all(bulk, valve)
+    greet(bulk, valve)
 
     for c in range(NVAR):
         hi, lo = split(field_ref[c].T)
@@ -303,28 +359,25 @@
     slot = lax.broadcasted_iota(jnp.int32, (1, CAP), 1)
     one, zero = jnp.ones((), bf16), jnp.zeros((), bf16)
 
-    def value_copy(owner, landing):
-        return pltpu.make_async_remote_copy(
-            src_ref=picked.at[owner],
-            dst_ref=arrived.at[landing],
-            send_sem=away_sem.at[owner],
-            recv_sem=home_sem.at[landing],
-            device_id=(owner // n_valve, lax.rem(owner, n_valve)),
-            device_id_type=MESH,
-        )
+    values = Exchange(
+        lambda v: picked.at[v], middle, lambda b: middle.at[:, b], arrived, value_sems
+    )
 
     def pick(part, carry):
-        first = lax.rem(bulk + part, n_bulk) * n_valve
+        steps = [part * ROWS + u + 1 for u in range(ROWS)]
+        rows_v = [lax.rem(valve + step, n_valve) for step in steps]
+        places = [(b, v) for v in rows_v for b in range(n_bulk)]
         hits, depths = [], []
-        for u in range(n_valve):
-            cell = cell_ref[first + u]
+        for b, v in places:
+            owner = b * n_valve + v
+            cell = cell_ref[owner]
             hits.append(jnp.where(plane_row == as_bf16(cell >> 7), one, zero))
-            depths.append(jnp.where(slot < count_ref[0, first + u], cell & (BZ - 1), -1))
+            depths.append(jnp.where(slot < count_ref[0, owner], cell & (BZ - 1), -1))
         hits = jnp.concatenate(hits, axis=1)
         columns = lax.dot_general(
             table[...], jnp.concatenate([hits, hits], axis=0), NN, preferred_element_type=f32
         )
-        for u in range(n_valve):
+        for u, (b, v) in enumerate(places):
             here = depth_row == depths[u]
             rows = [
                 jnp.sum(
@@ -334,34 +387,31 @@
                 )
                 for c in range(NVAR)
             ]
-            picked[first + u] = jnp.concatenate(rows, axis=0)
-
-        @pl.when(part == 0)
-        def _():
-            pl.semaphore_wait(pltpu.get_barrier_semaphore(), owners - 1)
-            arrived[me] = picked[me]
-
-        def send(v, carry):
-            owner = first + lax.rem(valve + v, n_valve)
-            pl.when(owner != me)(value_copy(owner, me).start)
-            return carry
-
-        return lax.fori_loop(0, n_valve, send, carry)
-
-    lax.fori_loop(0, n_bulk, pick, 0)
-
-    def terms(sender):
-        base = donor_ref[sender, 7:8].astype(jnp.int32)
+            picked[v, b] = jnp.concatenate(rows, axis=0)
+        pl.when(part == 0)(greeted)
+        for step in steps:
+            pl.when(step < n_valve)(lambda step=step: values.start_first(step))
+        return carry
+
+    lax.fori_loop(0, n_valve // ROWS, pick, 0)
+    middle[valve] = picked[valve]
+    values.finish_first()
+    values.start_second()
+    for v in range(n_valve):
+        arrived[bulk, v] = middle[v, bulk]
+
+    def terms(group, sender):
+        base = donor_ref[group, sender, 7:8].astype(jnp.int32)
         plane = base >> 7
         odd = (base & 1) == 1
-        weight = [donor_ref[sender, k : k + 1] for k in range(7)]
+        weight = [donor_ref[group, sender, k : k + 1] for k in range(7)]
         weight.append(1.0 - ((weight[0] + weight[1]) + (weight[2] + weight[3]) + (weight[4] + weight[5]) + weight[6]))
         rows = []
         for pair in range(4):
             near, deep = weight[2 * pair], weight[2 * pair + 1]
             rows += [jnp.where(odd, 0.0, near), jnp.where(odd, near, deep), jnp.where(odd, deep, 0.0)]
         weight_hi, weight_lo = split(jnp.concatenate(rows, axis=0))
-        value_hi, value_lo = split(arrived[sender])
+        value_hi, value_lo = split(arrived[group, sender])
         hits = [plane_row == as_bf16(plane + off) for off in (0, 1, BY, BY + 1)]
 
         def spread(weight):
@@ -383,15 +433,9 @@
         return spread(weight_hi), spread(weight_lo), placed(value_hi), placed(value_lo)
 
     def push(part, carry):
-        first = lax.rem(bulk - part + n_bulk, n_bulk) * n_valve
-
-        def land(v, carry):
-            sender = first + v
-            pl.when(sender != me)(value_copy(sender, sender).wait_recv)
-            return carry
-
-        lax.fori_loop(0, n_valve, land, 0)
-        parts = [terms(first + u) for u in range(n_valve)]
+        group = lax.rem(bulk - part + n_bulk, n_bulk)
+        pl.when(part > 0)(lambda: values.finish_second(group))
+        parts = [terms(group, v) for v in range(n_valve)]
         spread_hi, spread_lo, placed_hi, placed_lo = [
             jnp.concatenate([part[i] for part in parts], axis=1) for i in range(4)
         ]
@@ -411,42 +455,32 @@
             columns = slice(half * BZ, (half + 1) * BZ)
             mixed[half, pl.ds(0, PAIRS, stride=2), :] = even[:, columns]
             mixed[half, pl.ds(1, PAIRS, stride=2), :] = odd[:, columns]
-            out_ref[c, pl.ds(half * BZ, BZ), :] = swept_ref[c, pl.ds(half * BZ, BZ), :] + mixed[half].T
-
-    def left(owner, carry):
-        pl.when(owner != me)(value_copy(owner, me).wait_send)
-        return carry
-
-    lax.fori_loop(0, owners, left, 0)
-
-
-def donor_terms(field, cells, counts, donors, swept):
-    owners = cells.shape[0]
+            out_ref[c, pl.ds(half * BZ, BZ), :] = mixed[half].T
+
+    values.sent()
+
+
+def donor_terms(field, cells, counts, donors):
+    n_bulk, n_valve, _, _ = donors.shape
     whole = pl.BlockSpec(memory_space=pltpu.VMEM)
     return pl.pallas_call(
         donor_kernel,
         out_shape=jax.ShapeDtypeStruct((NVAR, PLANES, BZ), f32),
-        in_specs=[pl.BlockSpec(memory_space=pltpu.SMEM)] + [whole] * 4,
+        in_specs=[pl.BlockSpec(memory_space=pltpu.SMEM)] + [whole] * 3,
         out_specs=whole,
         scratch_shapes=[
             pltpu.VMEM((NVAR * BZ, 2 * PLANES), bf16),
-            pltpu.VMEM((owners, NVAR, CAP), f32),
-            pltpu.VMEM((owners, NVAR, CAP), f32),
+            pltpu.VMEM((n_valve, n_bulk, NVAR, CAP), f32),
+            pltpu.VMEM((n_valve, n_bulk, NVAR, CAP), f32),
+            pltpu.VMEM((n_bulk, n_valve, NVAR, CAP), f32),
             pltpu.VMEM((NVAR * PAIRS, 3 * PLANES), f32),
             pltpu.VMEM((PLANES // BZ, BZ, BZ), f32),
-            pltpu.SemaphoreType.DMA((owners,)),
-            pltpu.SemaphoreType.DMA((owners,)),
-        ],
+        ]
+        + exchange_sems(n_bulk, n_valve),
         compiler_params=pltpu.CompilerParams(
             collective_id=1, has_side_effects=True, vmem_limit_bytes=56 * 2**20
         ),
-    )(
-        counts,
-        cells.reshape(owners, 1, CAP),
-        field.reshape(NVAR, PLANES, BZ),
-        donors,
-        swept.reshape(NVAR, PLANES, BZ),
-    )
+    )(counts, cells.reshape(n_bulk * n_valve, 1, CAP), field.reshape(NVAR, PLANES, BZ), donors)
 
 
 def body(
@@ -475,7 +509,8 @@
         donor_weight[:, 0],
         donor_base[0],
     )
-    bg_out = donor_terms(valve_out, rec_cell[0], slot_count, donors, bg_swept).reshape(bg_adjoint.shape)
+    pushed = donor_terms(valve_out, rec_cell[0], slot_count, donors)
+    bg_out = bg_swept + pushed.reshape(bg_swept.shape)
     return (bg_out, valve_out)
 
 

time: 108 us -> 90.4 us (0.84)
  Pallas kernels: 102 us -> 85.2 us
  other arithmetic: 0 us -> 2.1 us
  local copies, waits for them, and re-layouts: 4.2 us -> 2.15 us
    pallas_call x1, Pallas kernels: 44.8 us -> 32.9 us  [sweep_grids(): pl.pallas_call(sweep_kernel, out_shape=(out, out, jax.ShapeDtypeStruct((n...]
    pallas_call x1, Pallas kernels: 57.2 us -> 52.3 us  [donor_terms(): pl.pallas_call(donor_kernel, out_shape=jax.ShapeDtypeStruct((NVAR, PLANES...]
    add x0 -> x1, other arithmetic: none -> 2.1 us  [body(): bg_out = bg_swept + pushed.reshape(bg_swept.shape)]
    unnamed x5 -> x6, local copies, waits for them, and re-layouts: 4.2 us -> 2.15 us
where the time goes in v2:
time: 90.4 us; the launch traced here: 90.2 us
  Pallas kernels  85.2 us (94%)
  local copies, waits for them, and re-layouts  2.15 us (2%)
  other arithmetic  2.1 us (2%)
    pallas_call x1, Pallas kernels, donor_terms(): pl.pallas_call(donor_kernel, out_shape=jax.ShapeDtypeStruct((NVAR, PLANES...  52.3 us
    pallas_call x1, Pallas kernels, sweep_grids(): pl.pallas_call(sweep_kernel, out_shape=(out, out, jax.ShapeDtypeStruct((n...  32.9 us
    unnamed x6, local copies, waits for them, and re-layouts  2.15 us
    add x1, other arithmetic, body(): bg_out = bg_swept + pushed.reshape(bg_swept.shape)  2.1 us

profile of v2, /device:TPU:0, one launch (start us, length us, event | category | flops | bytes accessed | tf_op | source)
XLA Modules:
  0.0 90.2 jit_solution(10549473611143728742)
XLA Ops:
  0.6 1.3 %copy.14.refs_0_ = f32[3,5,5]{2,1,0:T(8,128)} copy(f32[3,5,5]{2,0,1:T(4,128)} %param.19) | data formatting | bytes 600 | tf_op args[7]
  1.9 32.9 %shard_map.131 = (f32[5,8,32,128]{3,2,1,0:T(8,128)}, f32[5,8,32,128]{3,2,1,0:T(8,128)}, f32[8,16,8,128]{3,2,1,0:T(8,128)}) custom-call(f32[3,5,5]{2,1,0:T(8,128)} %copy.14.refs_0_, f32[5,8,32,128]{3,2,1,0:T(8,128)} %refs_1_.1, f32[3,8,32,128]{3,2,1,0:T(8,128)} %refs_2_.1, f32[5,8,32,128]{3,2,1,0:T(8,128)} %refs_3_.1, f32[5,8,32,128]{3,2,1,0:T(8,128)} %refs_4_.1, ...), custom_call_target="tpu_custom_call" | custom-call | tf_op jit(solution)/shard_map/pallas_call | solution.py:309
  34.8 0.0 copy-start.1
  34.9 52.3 %shard_map.132 = f32[5,256,128]{2,1,0:T(8,128)} custom-call(s32[1,128]{1,0:T(1,128)} %count_ref.1, s32[128,1,128]{2,1,0:T(1,128)} %bitcast.9, f32[5,256,128]{2,1,0:T(8,128)} %bitcast.5, f32[8,16,8,128]{3,2,1,0:T(8,128)} %get-tuple-element.7.donor_ref), custom_call_target="tpu_custom_call" | custom-call | tf_op jit(solution)/shard_map/pallas_call | solution.py:466
  87.2 0.0 copy-done.1
  87.2 0.0 copy-start
  87.2 2.1 %add.3 = f32[5,8,32,128]{3,2,1,0:T(8,128)} add(f32[5,8,32,128]{3,2,1,0:T(8,128)S(1)} %copy-done.1, f32[5,8,32,128]{3,2,1,0:T(8,128)} %bitcast.6) | non-fusion elementwise | flops 163840 | bytes 1966080 | tf_op jit(solution)/shard_map/add | solution.py:513
  89.3 0.0 copy-done
  89.3 0.8 copy.16
Async XLA Ops:
  34.8 52.4 %copy-start.1 = (f32[5,8,32,128]{3,2,1,0:T(8,128)S(1)}, f32[5,8,32,128]{3,2,1,0:T(8,128)}, u32[]{:S(2)}) copy-start(f32[5,8,32,128]{3,2,1,0:T(8,128)} %get-tuple-element.5) | copy-start | bytes 1966084
  87.2 2.1 %copy-start = (f32[5,8,32,128]{3,2,1,0:T(8,128)S(1)}, f32[5,8,32,128]{3,2,1,0:T(8,128)}, u32[]{:S(2)}) copy-start(f32[5,8,32,128]{3,2,1,0:T(8,128)} %get-tuple-element.11) | copy-start | bytes 1966084

commit v3 on v2

--- a/solution.py
+++ b/solution.py
@@ -99,25 +99,37 @@
     ]
 
 
-def sweep_kernel(*refs):
-    (flux_ref, valve_adj, valve_vel, valve_src, bg_adj, bg_vel, bg_src, bg_blank) = refs[:8]
-    (weight_ref, base_ref, valve_out, bg_out, donors_in) = refs[8:13]
-    fields = (refs[13 : 13 + ITERS], refs[13 + ITERS : 13 + 2 * ITERS])
-    (slopes, scale, edge_in, edge_out, mix, donors_out, donors_mid, load_sem, send_sem, recv_sem, own_sem) = refs[
-        13 + 2 * ITERS : 24 + 2 * ITERS
-    ]
-    donor_sems = refs[24 + 2 * ITERS :]
+def split(x):
+    hi = x.astype(bf16)
+    return hi, (x - hi.astype(f32)).astype(bf16)
+
+
+def as_bf16(x):
+    return x.astype(f32).astype(bf16)
+
+
+def step_kernel(*refs):
+    (flux_ref, count_ref, valve_adj, bg_adj) = refs[:4]
+    far, (valve_out, bg_out) = refs[4:12], refs[12:14]
+    fields = (refs[14 : 14 + ITERS], refs[14 + ITERS : 14 + 2 * ITERS])
+    (slopes, scale, edge_in, edge_out, mix, donors_out, donors_mid, donors_in) = refs[22:30]
+    (bg_swept, table, picked, middle, arrived, total, mixed) = refs[30:37]
+    near = refs[37:45]
+    (valve_vel, bg_vel, bg_blank, valve_src, bg_src, weight_ref, base_ref, cell_ref) = near
+    (load_sem, send_sem, recv_sem) = refs[45:48]
+    donor_sems, value_sems = refs[48:52], refs[52:56]
     bulk, valve = lax.axis_index("bulk"), lax.axis_index("valve")
     n_bulk, n_valve = lax.axis_size("bulk"), lax.axis_size("valve")
     place = {"bulk": (bulk, n_bulk), "valve": (valve, n_valve)}
     axes = (("valve", "bulk"), ("bulk", "valve"))
     inputs = ((valve_adj, valve_vel, valve_src), (bg_adj, bg_vel, bg_src))
-    outputs = (valve_out, bg_out)
+    outputs = (valve_out, bg_swept)
 
     loads = [
         pltpu.make_async_copy(inputs[g][0], fields[g][0].at[:, pl.ds(1, BX)], load_sem.at[g])
         for g in range(2)
     ]
+    loads += [pltpu.make_async_copy(far[k], near[k], load_sem.at[2 + k]) for k in range(len(near))]
     for load in loads:
         load.start()
 
@@ -251,6 +263,8 @@
 
         lax.fori_loop(0, BX, rows, 0)
 
+    loads[7].wait()
+    loads[8].wait()
     for b in range(n_bulk):
         owners = pl.ds(b * n_valve, n_valve)
         for k in range(7):
@@ -274,82 +288,27 @@
     for g in range(2):
         for kind in range(2):
             send(g, 0, kind)
-    for step in range(1, n_valve):
-        donors.start_first(step)
     donors_mid[valve] = donors_out[aligned(valve, n_bulk * 8)]
+    for k in (2, 3, 4):
+        loads[k].wait()
     lax.fori_loop(0, BX, slope_rows, 0)
     for d in range(3):
         for j in range(NVAR):
             for i in range(NVAR):
-                mix[(d * NVAR + j) * NVAR + i] = jnp.broadcast_to(flux_ref[d, j : j + 1, i : i + 1], (8, BZ))
-    own = pltpu.make_async_copy(donors.block(bulk), donors_in.at[bulk], own_sem)
+                mix[(d * NVAR + j) * NVAR + i] = jnp.broadcast_to(flux_ref[j, d : d + 1, i : i + 1], (8, BZ))
+    for k in (5, 6, 9):
+        loads[k].wait()
     for t in range(ITERS):
-        for g in range(2):
-            arrive(g, t)
-            sweep(g, t)
-        if t == 1:
-            donors.finish_first()
-            donors.start_second()
-            own.start()
-    own.wait()
-    for step in range(1, n_bulk):
-        donors.finish_second(lax.rem(bulk + step, n_bulk))
-    donors.sent()
-    for t in range(ITERS):
-        for g in range(2):
-            left(g, t)
-
-
-def sweep_grids(flux_mix, valve_adj, valve_vel, valve_src, bg_adj, bg_vel, bg_src, bg_blank, weights, base):
-    whole = pl.BlockSpec(memory_space=pltpu.VMEM)
-    far = pl.BlockSpec(memory_space=pl.ANY)
-    n_bulk, n_valve = lax.axis_size("bulk"), lax.axis_size("valve")
-    out = jax.ShapeDtypeStruct(valve_adj.shape, f32)
-    edges = pltpu.VMEM((2, ITERS, 2, NVAR, BX, 1, BZ), f32)
-    return pl.pallas_call(
-        sweep_kernel,
-        out_shape=(out, out, jax.ShapeDtypeStruct((n_bulk, n_valve, 8, CAP), f32)),
-        in_specs=[whole, far, whole, whole, far, whole, whole, whole, whole, whole],
-        out_specs=(whole, whole, far),
-        scratch_shapes=[pltpu.VMEM((NVAR, BX + 2, BY, BZ), f32)] * (2 * ITERS)
-        + [
-            pltpu.VMEM((2, 3, BX, BY, BZ), f32),
-            pltpu.VMEM((BX, BY, BZ), f32),
-            edges,
-            edges,
-            pltpu.VMEM((3 * NVAR * NVAR, 8, BZ), f32),
-            pltpu.VMEM((n_valve * n_bulk * 8, CAP), f32),
-            pltpu.VMEM((n_valve, n_bulk * 8, CAP), f32),
-            pltpu.SemaphoreType.DMA((2,)),
-            pltpu.SemaphoreType.DMA((2, ITERS, 2, 2)),
-            pltpu.SemaphoreType.DMA((2, ITERS, 2, 2)),
-            pltpu.SemaphoreType.DMA,
-        ]
-        + exchange_sems(n_bulk, n_valve),
-        compiler_params=pltpu.CompilerParams(
-            collective_id=0, has_side_effects=True, vmem_limit_bytes=56 * 2**20
-        ),
-    )(flux_mix, valve_adj, valve_vel, valve_src, bg_adj, bg_vel, bg_src, bg_blank, weights, base)
-
-
-def split(x):
-    hi = x.astype(bf16)
-    return hi, (x - hi.astype(f32)).astype(bf16)
-
-
-def as_bf16(x):
-    return x.astype(f32).astype(bf16)
-
-
-def donor_kernel(
-    count_ref, cell_ref, field_ref, donor_ref, out_ref, table, picked, middle, arrived, total, mixed, *value_sems
-):
-    bulk, valve = lax.axis_index("bulk"), lax.axis_index("valve")
-    n_bulk, n_valve = lax.axis_size("bulk"), lax.axis_size("valve")
-    greet(bulk, valve)
-
+        arrive(0, t)
+        sweep(0, t)
+        if t + 1 < ITERS:
+            arrive(1, t)
+            sweep(1, t)
+
+    for step in range(1, n_valve):
+        donors.start_first(step)
     for c in range(NVAR):
-        hi, lo = split(field_ref[c].T)
+        hi, lo = split(valve_out[c].reshape(PLANES, BZ).T)
         table[pl.ds(c * BZ, BZ), 0:PLANES] = hi
         table[pl.ds(c * BZ, BZ), PLANES : 2 * PLANES] = lo
     total[...] = jnp.zeros_like(total)
@@ -388,23 +347,30 @@
                 for c in range(NVAR)
             ]
             picked[v, b] = jnp.concatenate(rows, axis=0)
-        pl.when(part == 0)(greeted)
         for step in steps:
             pl.when(step < n_valve)(lambda step=step: values.start_first(step))
         return carry
 
-    lax.fori_loop(0, n_valve // ROWS, pick, 0)
+    parts = n_valve // ROWS
+    lax.fori_loop(0, parts // 2, pick, 0)
+    donors.finish_first()
+    donors.start_second()
+    for v in range(n_valve):
+        donors_in[bulk, v] = donors_mid[v, aligned(bulk, 8)]
+    lax.fori_loop(parts // 2, parts, pick, 0)
     middle[valve] = picked[valve]
+    arrive(1, ITERS - 1)
+    sweep(1, ITERS - 1)
     values.finish_first()
     values.start_second()
     for v in range(n_valve):
         arrived[bulk, v] = middle[v, bulk]
 
     def terms(group, sender):
-        base = donor_ref[group, sender, 7:8].astype(jnp.int32)
+        base = donors_in[group, sender, 7:8].astype(jnp.int32)
         plane = base >> 7
         odd = (base & 1) == 1
-        weight = [donor_ref[group, sender, k : k + 1] for k in range(7)]
+        weight = [donors_in[group, sender, k : k + 1] for k in range(7)]
         weight.append(1.0 - ((weight[0] + weight[1]) + (weight[2] + weight[3]) + (weight[4] + weight[5]) + weight[6]))
         rows = []
         for pair in range(4):
@@ -434,10 +400,15 @@
 
     def push(part, carry):
         group = lax.rem(bulk - part + n_bulk, n_bulk)
-        pl.when(part > 0)(lambda: values.finish_second(group))
-        parts = [terms(group, v) for v in range(n_valve)]
+
+        @pl.when(part > 0)
+        def _():
+            donors.finish_second(group)
+            values.finish_second(group)
+
+        found = [terms(group, v) for v in range(n_valve)]
         spread_hi, spread_lo, placed_hi, placed_lo = [
-            jnp.concatenate([part[i] for part in parts], axis=1) for i in range(4)
+            jnp.concatenate([one[i] for one in found], axis=1) for i in range(4)
         ]
         both = lax.dot_general(
             jnp.concatenate([placed_hi, placed_lo], axis=0), spread_hi, NT, preferred_element_type=f32
@@ -455,20 +426,39 @@
             columns = slice(half * BZ, (half + 1) * BZ)
             mixed[half, pl.ds(0, PAIRS, stride=2), :] = even[:, columns]
             mixed[half, pl.ds(1, PAIRS, stride=2), :] = odd[:, columns]
-            out_ref[c, pl.ds(half * BZ, BZ), :] = mixed[half].T
+            here = pl.ds(half * (BX // 2), BX // 2)
+            bg_out[c, here] = bg_swept[c, here] + mixed[half].T.reshape(BX // 2, BY, BZ)
 
     values.sent()
-
-
-def donor_terms(field, cells, counts, donors):
-    n_bulk, n_valve, _, _ = donors.shape
+    donors.sent()
+    for t in range(ITERS):
+        for g in range(2):
+            left(g, t)
+
+
+def whole_step(flux_mix, counts, valve_adj, bg_adj, *rest):
     whole = pl.BlockSpec(memory_space=pltpu.VMEM)
+    far = pl.BlockSpec(memory_space=pltpu.HBM)
+    small = pl.BlockSpec(memory_space=pltpu.SMEM)
+    n_bulk, n_valve = lax.axis_size("bulk"), lax.axis_size("valve")
+    out = jax.ShapeDtypeStruct(valve_adj.shape, f32)
+    edges = pltpu.VMEM((2, ITERS, 2, NVAR, BX, 1, BZ), f32)
     return pl.pallas_call(
-        donor_kernel,
-        out_shape=jax.ShapeDtypeStruct((NVAR, PLANES, BZ), f32),
-        in_specs=[pl.BlockSpec(memory_space=pltpu.SMEM)] + [whole] * 3,
-        out_specs=whole,
-        scratch_shapes=[
+        step_kernel,
+        out_shape=(out, out),
+        in_specs=[whole, small] + [far] * 10,
+        out_specs=(whole, whole),
+        scratch_shapes=[pltpu.VMEM((NVAR, BX + 2, BY, BZ), f32)] * (2 * ITERS)
+        + [
+            pltpu.VMEM((2, 3, BX, BY, BZ), f32),
+            pltpu.VMEM((BX, BY, BZ), f32),
+            edges,
+            edges,
+            pltpu.VMEM((3 * NVAR * NVAR, 8, BZ), f32),
+            pltpu.VMEM((n_valve * n_bulk * 8, CAP), f32),
+            pltpu.VMEM((n_valve, n_bulk * 8, CAP), f32),
+            pltpu.VMEM((n_bulk, n_valve, 8, CAP), f32),
+            pltpu.VMEM((NVAR, BX, BY, BZ), f32),
             pltpu.VMEM((NVAR * BZ, 2 * PLANES), bf16),
             pltpu.VMEM((n_valve, n_bulk, NVAR, CAP), f32),
             pltpu.VMEM((n_valve, n_bulk, NVAR, CAP), f32),
@@ -476,11 +466,17 @@
             pltpu.VMEM((NVAR * PAIRS, 3 * PLANES), f32),
             pltpu.VMEM((PLANES // BZ, BZ, BZ), f32),
         ]
-        + exchange_sems(n_bulk, n_valve),
+        + [pltpu.VMEM(x.shape, x.dtype) for x in rest]
+        + [
+            pltpu.SemaphoreType.DMA((2 + len(rest),)),
+            pltpu.SemaphoreType.DMA((2, ITERS, 2, 2)),
+            pltpu.SemaphoreType.DMA((2, ITERS, 2, 2)),
+        ]
+        + exchange_sems(n_bulk, n_valve) * 2,
         compiler_params=pltpu.CompilerParams(
-            collective_id=1, has_side_effects=True, vmem_limit_bytes=56 * 2**20
+            collective_id=0, has_side_effects=True, vmem_limit_bytes=56 * 2**20
         ),
-    )(counts, cells.reshape(n_bulk * n_valve, 1, CAP), field.reshape(NVAR, PLANES, BZ), donors)
+    )(flux_mix, counts, valve_adj, bg_adj, *rest)
 
 
 def body(
@@ -497,20 +493,21 @@
     donor_weight,
     slot_count,
 ):
-    valve_out, bg_swept, donors = sweep_grids(
-        flux_mix,
+    n_owners = rec_cell.shape[1]
+    valve_out, bg_out = whole_step(
+        flux_mix.transpose(1, 0, 2),
+        slot_count,
         valve_adjoint,
+        bg_adjoint,
         valve_velocity,
+        bg_velocity,
+        bg_iblank,
         valve_source,
-        bg_adjoint,
-        bg_velocity,
         bg_source,
-        bg_iblank,
         donor_weight[:, 0],
         donor_base[0],
+        rec_cell.reshape(n_owners, 1, CAP),
     )
-    pushed = donor_terms(valve_out, rec_cell[0], slot_count, donors)
-    bg_out = bg_swept + pushed.reshape(bg_swept.shape)
     return (bg_out, valve_out)
 
 

time: 90.4 us -> 82.4 us (0.912)
  Pallas kernels: 85.2 us -> 78.6 us
  other arithmetic: 2.1 us -> 0 us
    pallas_call x2 -> x1, Pallas kernels: 85.2 us -> 78.6 us  [whole_step(): pl.pallas_call(step_kernel, out_shape=(out, out), in_specs=[whole, small]...]
    add x1 -> x0, other arithmetic: 2.1 us -> none  [body(): bg_out = bg_swept + pushed.reshape(bg_swept.shape)]
    unnamed x6 -> x4, local copies, waits for them, and re-layouts: 2.15 us -> 2.89 us
where the time goes in v3:
time: 82.4 us; the launch traced here: 82.2 us
  Pallas kernels  78.6 us (95%)
  local copies, waits for them, and re-layouts  2.89 us (4%)
    pallas_call x1, Pallas kernels, whole_step(): pl.pallas_call(step_kernel, out_shape=(out, out), in_specs=[whole, small]...  78.6 us
    unnamed x4, local copies, waits for them, and re-layouts  2.89 us

profile of v3, /device:TPU:0, one launch (start us, length us, event | category | flops | bytes accessed | tf_op | source)
XLA Modules:
  0.0 82.2 jit_solution(11383830977981830895)
XLA Ops:
  0.6 78.6 %shard_map.131 = (f32[5,8,32,128]{3,2,1,0:T(8,128)}, f32[5,8,32,128]{3,2,1,0:T(8,128)}) custom-call(f32[5,3,5]{2,1,0:T(4,128)} %bitcast.7, s32[1,128]{1,0:T(1,128)} %refs_1_.1, f32[5,8,32,128]{3,2,1,0:T(8,128)} %refs_2_.1, f32[5,8,32,128]{3,2,1,0:T(8,128)} %refs_3_.1, f32[3,8,32,128]{3,2,1,0:T(8,128)} %refs_4_.1, f32[3,8,32,128]{3,2,1,0:T(8,128)} %refs_5_.1, ...), custom_call_target="tpu_custom_call" | custom-call | tf_op jit(solution)/shard_map/pallas_call | solution.py:446
  79.3 0.0 copy-start
  79.3 2.1 %copy.16 = f32[5,8,32,128]{3,2,1,0:T(8,128)} copy(f32[5,8,32,128]{3,2,1,0:T(8,128)} %get-tuple-element.8) | data formatting | bytes 1310720
  81.3 0.0 copy-done
  81.3 0.8 %copy.17 = f32[5,8,32,128]{3,2,1,0:T(8,128)} copy(f32[5,8,32,128]{3,2,1,0:T(8,128)S(1)} %copy-done) | data formatting | bytes 1310720
Async XLA Ops:
  79.3 2.1 %copy-start = (f32[5,8,32,128]{3,2,1,0:T(8,128)S(1)}, f32[5,8,32,128]{3,2,1,0:T(8,128)}, u32[]{:S(2)}) copy-start(f32[5,8,32,128]{3,2,1,0:T(8,128)} %get-tuple-element.9) | copy-start | bytes 1966084

commit v4 on v3

--- a/solution.py
+++ b/solution.py
@@ -129,9 +129,9 @@
         pltpu.make_async_copy(inputs[g][0], fields[g][0].at[:, pl.ds(1, BX)], load_sem.at[g])
         for g in range(2)
     ]
-    loads += [pltpu.make_async_copy(far[k], near[k], load_sem.at[2 + k]) for k in range(len(near))]
     for load in loads:
         load.start()
+    loads += [pltpu.make_async_copy(far[k], near[k], load_sem.at[2 + k]) for k in range(len(near))]
 
     def clear(g, side):
         index, count = place[axes[g][0]]
@@ -263,14 +263,6 @@
 
         lax.fori_loop(0, BX, rows, 0)
 
-    loads[7].wait()
-    loads[8].wait()
-    for b in range(n_bulk):
-        owners = pl.ds(b * n_valve, n_valve)
-        for k in range(7):
-            donors_out[pl.ds(b * 8 + k, n_valve, stride=n_bulk * 8), :] = weight_ref[k, owners]
-        donors_out[pl.ds(b * 8 + 7, n_valve, stride=n_bulk * 8), :] = base_ref[owners].astype(f32)
-
     def aligned(index, size):
         return pl.ds(pl.multiple_of(index * size, size), size)
 
@@ -284,14 +276,23 @@
     for g in range(2):
         loads[g].wait()
         first_edges(g)
+    for load in loads[2:]:
+        load.start()
     greeted()
     for g in range(2):
         for kind in range(2):
             send(g, 0, kind)
-    donors_mid[valve] = donors_out[aligned(valve, n_bulk * 8)]
     for k in (2, 3, 4):
         loads[k].wait()
     lax.fori_loop(0, BX, slope_rows, 0)
+    loads[7].wait()
+    loads[8].wait()
+    for b in range(n_bulk):
+        owners = pl.ds(b * n_valve, n_valve)
+        for k in range(7):
+            donors_out[pl.ds(b * 8 + k, n_valve, stride=n_bulk * 8), :] = weight_ref[k, owners]
+        donors_out[pl.ds(b * 8 + 7, n_valve, stride=n_bulk * 8), :] = base_ref[owners].astype(f32)
+    donors_mid[valve] = donors_out[aligned(valve, n_bulk * 8)]
     for d in range(3):
         for j in range(NVAR):
             for i in range(NVAR):
@@ -307,6 +308,7 @@
 
     for step in range(1, n_valve):
         donors.start_first(step)
+
     for c in range(NVAR):
         hi, lo = split(valve_out[c].reshape(PLANES, BZ).T)
         table[pl.ds(c * BZ, BZ), 0:PLANES] = hi
@@ -398,15 +400,8 @@
 
         return spread(weight_hi), spread(weight_lo), placed(value_hi), placed(value_lo)
 
-    def push(part, carry):
-        group = lax.rem(bulk - part + n_bulk, n_bulk)
-
-        @pl.when(part > 0)
-        def _():
-            donors.finish_second(group)
-            values.finish_second(group)
-
-        found = [terms(group, v) for v in range(n_valve)]
+    def push(groups):
+        found = [terms(group, v) for group in groups for v in range(n_valve)]
         spread_hi, spread_lo, placed_hi, placed_lo = [
             jnp.concatenate([one[i] for one in found], axis=1) for i in range(4)
         ]
@@ -415,9 +410,21 @@
         )
         low = lax.dot_general(placed_hi, spread_lo, NT, preferred_element_type=f32)
         total[...] += both[: NVAR * PAIRS] + both[NVAR * PAIRS :] + low
+
+    def landed(step):
+        group = lax.rem(bulk - step + n_bulk, n_bulk)
+        donors.finish_second(group)
+        values.finish_second(group)
+        return group
+
+    def push_two(pair, carry):
+        push([landed(2 * pair + 1), landed(2 * pair + 2)])
         return carry
 
-    lax.fori_loop(0, n_bulk, push, 0)
+    push([bulk])
+    lax.fori_loop(0, (n_bulk - 1) // 2, push_two, 0)
+    if n_bulk % 2 == 0:
+        push([landed(n_bulk - 1)])
     for c in range(NVAR):
         rows = pl.ds(c * PAIRS, PAIRS)
         even = total[rows, 0:PLANES] + pltpu.roll(total[rows, 2 * PLANES : 3 * PLANES], 1, axis=0)

time: 82.4 us -> 81.5 us (0.989)
    pallas_call x1, Pallas kernels: 78.6 us -> 77.8 us  [whole_step(): pl.pallas_call(step_kernel, out_shape=(out, out), in_specs=[whole, small]...]
where the time goes in v4:
time: 81.5 us; the launch traced here: 81.3 us
  Pallas kernels  77.8 us (95%)
  local copies, waits for them, and re-layouts  2.89 us (4%)
    pallas_call x1, Pallas kernels, whole_step(): pl.pallas_call(step_kernel, out_shape=(out, out), in_specs=[whole, small]...  77.8 us
    unnamed x4, local copies, waits for them, and re-layouts  2.89 us

profile of v4, /device:TPU:0, one launch (start us, length us, event | category | flops | bytes accessed | tf_op | source)
XLA Modules:
  0.0 81.3 jit_solution(2833673259276383754)
XLA Ops:
  0.6 77.8 %shard_map.131 = (f32[5,8,32,128]{3,2,1,0:T(8,128)}, f32[5,8,32,128]{3,2,1,0:T(8,128)}) custom-call(f32[5,3,5]{2,1,0:T(4,128)} %bitcast.7, s32[1,128]{1,0:T(1,128)} %refs_1_.1, f32[5,8,32,128]{3,2,1,0:T(8,128)} %refs_2_.1, f32[5,8,32,128]{3,2,1,0:T(8,128)} %refs_3_.1, f32[3,8,32,128]{3,2,1,0:T(8,128)} %refs_4_.1, f32[3,8,32,128]{3,2,1,0:T(8,128)} %refs_5_.1, ...), custom_call_target="tpu_custom_call" | custom-call | tf_op jit(solution)/shard_map/pallas_call | solution.py:453
  78.4 0.0 copy-start
  78.4 2.1 %copy.16 = f32[5,8,32,128]{3,2,1,0:T(8,128)} copy(f32[5,8,32,128]{3,2,1,0:T(8,128)} %get-tuple-element.8) | data formatting | bytes 1310720
  80.5 0.0 copy-done
  80.5 0.8 %copy.17 = f32[5,8,32,128]{3,2,1,0:T(8,128)} copy(f32[5,8,32,128]{3,2,1,0:T(8,128)S(1)} %copy-done) | data formatting | bytes 1310720
Async XLA Ops:
  78.4 2.1 %copy-start = (f32[5,8,32,128]{3,2,1,0:T(8,128)S(1)}, f32[5,8,32,128]{3,2,1,0:T(8,128)}, u32[]{:S(2)}) copy-start(f32[5,8,32,128]{3,2,1,0:T(8,128)} %get-tuple-element.9) | copy-start | bytes 1966084

commit v5 on v4

--- a/solution.py
+++ b/solution.py
@@ -486,6 +486,42 @@
     )(flux_mix, counts, valve_adj, bg_adj, *rest)
 
 
+def hand_kernel(valve_ref, bg_ref, valve_out, bg_out, held, in_sem, out_sem):
+    steps = []
+    for g, (source, target) in enumerate(((valve_ref, valve_out), (bg_ref, bg_out))):
+        for c in range(NVAR):
+            steps.append(
+                (
+                    pltpu.make_async_copy(source.at[c], held.at[g, c], in_sem.at[g, c]),
+                    pltpu.make_async_copy(held.at[g, c], target.at[c], out_sem.at[g, c]),
+                )
+            )
+    for come, _ in steps:
+        come.start()
+    for come, go in steps:
+        come.wait()
+        go.start()
+    for _, go in steps:
+        go.wait()
+
+
+def hand_over(valve, bg):
+    far = pl.BlockSpec(memory_space=pl.ANY)
+    out = jax.ShapeDtypeStruct(valve.shape, f32)
+    return pl.pallas_call(
+        hand_kernel,
+        out_shape=(out, out),
+        in_specs=[far, far],
+        out_specs=(far, far),
+        scratch_shapes=[
+            pltpu.VMEM((2,) + valve.shape, f32),
+            pltpu.SemaphoreType.DMA((2, NVAR)),
+            pltpu.SemaphoreType.DMA((2, NVAR)),
+        ],
+        compiler_params=pltpu.CompilerParams(vmem_limit_bytes=56 * 2**20),
+    )(valve, bg)
+
+
 def body(
     bg_adjoint,
     bg_velocity,
@@ -515,6 +551,7 @@
         donor_base[0],
         rec_cell.reshape(n_owners, 1, CAP),
     )
+    valve_out, bg_out = hand_over(valve_out, bg_out)
     return (bg_out, valve_out)
 
 

time: 81.5 us -> 81 us (level)
  local copies, waits for them, and re-layouts: 2.89 us -> 0 us
  Pallas kernels: 77.8 us -> 80 us
    unnamed x4 -> x0, local copies, waits for them, and re-layouts: 2.89 us -> none
    pallas_call x0 -> x1, Pallas kernels: none -> 2.21 us  [hand_over(): pl.pallas_call(hand_kernel, out_shape=(out, out), in_specs=[far, far], ou...]
where the time goes in v5:
time: 81 us; the launch traced here: 80.8 us
  Pallas kernels  80 us (99%)
  between operations  0.82 us (1%)
    pallas_call x1, Pallas kernels, whole_step(): pl.pallas_call(step_kernel, out_shape=(out, out), in_specs=[whole, small]...  77.8 us
    pallas_call x1, Pallas kernels, hand_over(): pl.pallas_call(hand_kernel, out_shape=(out, out), in_specs=[far, far], ou...  2.21 us

profile of v5, /device:TPU:0, one launch (start us, length us, event | category | flops | bytes accessed | tf_op | source)
XLA Modules:
  0.0 80.8 jit_solution(2031776826146998048)
XLA Ops:
  0.6 77.8 %shard_map.131 = (f32[5,8,32,128]{3,2,1,0:T(8,128)}, f32[5,8,32,128]{3,2,1,0:T(8,128)}) custom-call(f32[5,3,5]{2,1,0:T(4,128)} %bitcast.7, s32[1,128]{1,0:T(1,128)} %refs_1_.1, f32[5,8,32,128]{3,2,1,0:T(8,128)} %refs_2_.1, f32[5,8,32,128]{3,2,1,0:T(8,128)} %refs_3_.1, f32[3,8,32,128]{3,2,1,0:T(8,128)} %refs_4_.1, f32[3,8,32,128]{3,2,1,0:T(8,128)} %refs_5_.1, ...), custom_call_target="tpu_custom_call" | custom-call | tf_op jit(solution)/shard_map/pallas_call | solution.py:453
  78.4 2.2 %shard_map.132 = (f32[5,8,32,128]{3,2,1,0:T(8,128)}, f32[5,8,32,128]{3,2,1,0:T(8,128)}) custom-call(f32[5,8,32,128]{3,2,1,0:T(8,128)} %get-tuple-element.6.valve_ref, f32[5,8,32,128]{3,2,1,0:T(8,128)} %get-tuple-element.7.bg_ref), custom_call_target="tpu_custom_call" | custom-call | tf_op jit(solution)/shard_map/pallas_call | solution.py:511
